TPU v7x, 512 devices: a whole 4x8x8 slice. The times are simulated.
512 devices in a mesh: dp: 64 (over y, z), tensor: 8 (over x, core).
Axes of the slice: x: 4, y: 8, z: 8, core: 2. Of those that a mesh axis runs over, the one named last changes fastest.
Arguments:
- activations: bfloat16 [81920, 5120], P('dp', 'tensor'), may hold values from -6 to 6
- cotangents: bfloat16 [81920, 1024], P('dp', 'tensor'), as said below
- error_old: bfloat16 [327680, 1024], P(('dp', 'tensor')), may hold values from -3 to 3
- pause_positions: int32 [320], replicated, may hold values from 0 to 1279, as said below
- initial_q: float32 [1024, 32], replicated, may hold values from -6 to 6
Outputs:
- error_new: bfloat16 [327680, 1024], P(('dp', 'tensor'))
- q_factor: float32 [1024, 32], P('tensor')
Inputs may be any that keep to these rules, and one draw needn't show every extreme that they name: pause_positions holds 320 different padding positions of a replica's batch, which attention masks out, in no particular order; they are the same for every replica. cotangents lie within 6 / sqrt(1280) in magnitude.
All inputs are finite; a program needn't handle non-finite values.
Results may differ from a plain program's by a relative error of at most 0.002.
Values may be sent and summed in bfloat16 or wider, within the bound.
No kernel may reach another device: no remote copies, remote signals or barrier semaphores. Data moves between devices by JAX's collectives and lax.ppermute only.
A program may use at most 64 MiB of HBM per device.

v0:
```python
import functools

import jax
import jax.numpy as jnp
from jax import lax
from jax.experimental import pallas as pl
from jax.experimental.pallas import tpu as pltpu
from jax.sharding import Mesh
from jax.sharding import PartitionSpec as P

DP = ("y", "z")
TENSOR = ("x", "c")
CHUNK = 256
LANES = 128
MIB = 1024 * 1024
F32 = jnp.float32
BF16 = jnp.bfloat16


def dot(a, b, contract, precision=None):
    return lax.dot_general(
        a, b, (contract, ((), ())), precision=precision, preferred_element_type=F32
    )


def params(limit=20 * MIB):
    return pltpu.CompilerParams(vmem_limit_bytes=limit)


def split(x):
    high = x.astype(BF16)
    return high, (x - high.astype(F32)).astype(BF16)


def selection(pauses, row_count, kept_count):
    count = pauses.shape[1]
    row = lax.broadcasted_iota(jnp.int32, (count, count), 0)
    col = lax.broadcasted_iota(jnp.int32, (count, count), 1)
    column = jnp.sum(
        jnp.where(row == col, pauses.astype(F32), 0.0), axis=1, keepdims=True
    )
    spot = lax.broadcasted_iota(jnp.int32, (1, row_count), 1).astype(F32)
    before = jnp.sum(jnp.where(column < spot, 1.0, 0.0), axis=0, keepdims=True)
    struck = jnp.sum(jnp.where(column == spot, 1.0, 0.0), axis=0, keepdims=True)
    target = jnp.where(struck > 0.0, -1.0, spot - before)
    rank = lax.broadcasted_iota(jnp.int32, (kept_count, row_count), 0).astype(F32)
    return jnp.where(rank == target, 1.0, 0.0).astype(BF16)


def compact_cotangents_kernel(pause_ref, cot_ref, out_ref):
    pick = selection(pause_ref[...], cot_ref.shape[0], out_ref.shape[1])
    kept = dot(pick, cot_ref[...], ((1,), (0,))).astype(BF16)
    for copy in range(out_ref.shape[0]):
        out_ref[copy] = kept


def compact_features_kernel(kept_count, pause_ref, act_ref, out_ref):
    pick = selection(pause_ref[...], act_ref.shape[0], kept_count)
    kept = dot(pick, act_ref[...], ((1,), (0,)))
    spare = jnp.zeros((out_ref.shape[1] - kept_count, kept.shape[1]), F32)
    out_ref[...] = jnp.concatenate([kept, spare], axis=0).T.astype(BF16)


def merge_kernel(feat_ref, own_ref, other_ref, err_ref, q_ref, merged_ref, left_ref):
    first = lax.axis_index("c") == 0
    pieces, kept_count, lanes = own_ref.shape
    rank = q_ref.shape[0]
    features, padded_count = feat_ref.shape
    q_high, q_low = split(q_ref[...])
    total = jnp.zeros((features, LANES), F32)
    for piece in range(pieces):
        own, other = own_ref[piece], other_ref[piece]
        cots = jnp.concatenate([jnp.where(first, own, other), jnp.where(first, other, own)], axis=1)
        cots = jnp.concatenate([cots, jnp.zeros((padded_count - kept_count, CHUNK), BF16)], axis=0)
        here = slice(piece * CHUNK, (piece + 1) * CHUNK)
        merged = dot(feat_ref[...], cots, ((1,), (0,))) + err_ref[:, here].astype(F32)
        merged_ref[:, here] = merged
        m_high, m_low = split(merged)
        high, low = q_high[:, here], q_low[:, here]
        upper = jnp.concatenate([high, high], axis=1)
        lower = jnp.concatenate([low, jnp.zeros_like(low)], axis=1)
        spare = jnp.zeros((LANES - 2 * rank, 2 * CHUNK), BF16)
        total += dot(
            jnp.concatenate([m_high, m_low], axis=1),
            jnp.concatenate([upper, lower, spare], axis=0),
            ((1,), (1,)),
        )
    turned = total.T
    left = (turned[:rank] + turned[rank : 2 * rank]).astype(BF16)
    for copy in range(left_ref.shape[0]):
        left_ref[copy] = left


def add_copies_kernel(in_ref, out_ref):
    total = in_ref[0].astype(F32)
    for copy in range(1, in_ref.shape[0]):
        total += in_ref[copy].astype(F32)
    total = total.astype(out_ref.dtype)
    for copy in range(out_ref.shape[0]):
        out_ref[copy] = total


def pack(gram, lines):
    rank = gram.shape[0]
    wide = jnp.concatenate([gram, jnp.zeros((rank, LANES - rank), F32)], axis=1)
    total = wide[:lines]
    for block in range(1, rank // lines):
        total += pltpu.roll(wide[block * lines : (block + 1) * lines], block * rank, 1)
    return total


def unpack(packed, rank):
    lines = packed.shape[0]
    blocks = [packed[:, :rank]]
    for block in range(1, rank // lines):
        blocks.append(pltpu.roll(packed, LANES - block * rank, 1)[:, :rank])
    return jnp.concatenate(blocks, axis=0)


def project_kernel(replicas, in_ref, merged_ref, left_ref, out_ref):
    rank = left_ref.shape[0]
    pieces, lines, lanes = out_ref.shape
    wide = CHUNK // lanes
    total = in_ref[0].astype(F32)
    for copy in range(1, in_ref.shape[0]):
        total += in_ref[copy].astype(F32)
    total = total / replicas
    left_ref[...] = total
    high, low = split(total)
    stack = jnp.concatenate([high, low], axis=0)
    gram = dot(total, total, ((1,), (1,)), lax.Precision.HIGHEST)
    packed = pack(gram, lines - rank)
    for chunk in range(pieces // wide):
        m_high, m_low = split(merged_ref[:, chunk * CHUNK : (chunk + 1) * CHUNK])
        both = dot(stack, m_high, ((1,), (0,)))
        part = both[:rank] + both[rank:] + dot(high, m_low, ((1,), (0,)))
        for piece in range(wide):
            here = chunk * wide + piece
            out_ref[here, :rank] = part[:, piece * lanes : (piece + 1) * lanes]
            out_ref[here, rank:] = packed


def add_blocks_kernel(rank, in_ref, out_ref, gram_ref):
    total = in_ref[0]
    for copy in range(1, in_ref.shape[0]):
        total += in_ref[copy]
    for copy in range(out_ref.shape[0]):
        out_ref[copy] = total[:rank]
    gram_ref[...] = total[rank:]


def inverse_factor(gram):
    rank = gram.shape[0]
    row = lax.broadcasted_iota(jnp.int32, (rank, rank), 0)
    col = lax.broadcasted_iota(jnp.int32, (rank, rank), 1)
    table = jnp.concatenate([gram, jnp.where(row == col, 1.0, 0.0)], axis=1)
    line = lax.broadcasted_iota(jnp.int32, (rank, 1), 0)
    for k in range(0, rank, 2):
        column, second = table[:, k : k + 1], table[:, k + 1 : k + 2]
        inverse = 1.0 / column[k : k + 1]
        slope = column[k + 1 : k + 2] * inverse
        pivot = second[k + 1 : k + 2] - slope * second[k : k + 1]
        top = table[k : k + 1, :]
        bottom = table[k + 1 : k + 2, :] - slope * top
        below = line > k + 1
        upper = jnp.where(below, column * inverse, 0.0)
        lower = jnp.where(below, (second - slope * column) / pivot, 0.0)
        table = jnp.where(line == k + 1, bottom, table - upper * top - lower * bottom)
    diagonal = jnp.sum(jnp.where(row == col, table[:, :rank], 0.0), axis=1, keepdims=True)
    return table[:, rank:] / jnp.sqrt(diagonal)


def finish_kernel(replicas, in_ref, gram_ref, left_ref, merged_ref, err_hbm, own_ref, q_ref, err_ref, sems):
    rank, width = q_ref.shape
    inverse = inverse_factor(unpack(gram_ref[...], rank))
    raw = jnp.concatenate([in_ref[piece] for piece in range(in_ref.shape[0])], axis=1)
    q_new = dot(inverse, raw / replicas, ((1,), (0,)), lax.Precision.HIGHEST)
    basis = dot(inverse, left_ref[...], ((1,), (0,)), lax.Precision.HIGHEST)
    q_ref[...] = q_new
    lanes = own_ref.shape[1]
    place = lax.axis_index("x") * lax.axis_size("c") + lax.axis_index("c")
    own_ref[...] = q_ref[:, pl.ds(pl.multiple_of(place * lanes, lanes), lanes)]
    high, low = split(q_new)
    stack = jnp.concatenate([high, high, low, jnp.zeros_like(high)], axis=0)
    high, low = split(basis)
    high = high.astype(F32)
    low = low.astype(F32)
    turned = jnp.concatenate([high, low, high, jnp.zeros_like(high)], axis=0).T.astype(BF16)
    stores = []
    chunks, rows, _ = err_ref.shape
    for chunk in range(chunks):
        here = slice(chunk * rows, (chunk + 1) * rows)
        update = dot(turned[here], stack, ((1,), (0,)))
        err_ref[chunk] = (merged_ref[here] - update).astype(BF16)
        stores.append(
            pltpu.make_async_copy(
                err_ref.at[chunk], err_hbm.at[pl.ds(chunk * rows, rows)], sems.at[chunk]
            )
        )
        stores[-1].start()
    for store in stores:
        store.wait()


def in_hbm():
    return pl.BlockSpec(memory_space=pltpu.HBM)


def whole(shape):
    return pl.BlockSpec(shape, lambda *_: (0,) * len(shape))


def to_all(pieces, axes):
    return lax.all_to_all(pieces, axes, split_axis=0, concat_axis=0, tiled=True)


def add_copies(x, count, dtype):
    return pl.pallas_call(
        add_copies_kernel,
        out_shape=jax.ShapeDtypeStruct((count, *x.shape[1:]), dtype),
        compiler_params=params(),
        name="add_copies",
    )(x)


def body(activations, cotangents, error_old, pause_positions, initial_q):
    row_count, features = activations.shape
    lanes = cotangents.shape[1]
    width, rank = initial_q.shape
    kept_count = row_count - pause_positions.shape[0]
    padded_count = -(-kept_count // CHUNK) * CHUNK
    replicas = lax.axis_size(DP)
    line_x, across = lax.axis_size("x"), lax.axis_size("z")
    crowd = lax.axis_size(TENSOR)
    chunks = width // CHUNK
    lines = rank * rank // LANES
    pauses = pause_positions.reshape(1, -1)

    cot_copies = pl.pallas_call(
        compact_cotangents_kernel,
        out_shape=jax.ShapeDtypeStruct((line_x, kept_count, lanes), BF16),
        compiler_params=params(),
        name="compact_cotangents",
    )(pauses, cotangents)
    own = to_all(cot_copies, "x")
    kept_features = pl.pallas_call(
        functools.partial(compact_features_kernel, kept_count),
        out_shape=jax.ShapeDtypeStruct((features, padded_count), BF16),
        compiler_params=params(),
        cost_estimate=pl.CostEstimate(
            flops=2 * kept_count * row_count * features,
            bytes_accessed=4 * row_count * features,
            transcendentals=0,
        ),
        name="compact_features",
    )(pauses, activations)
    cores = lax.axis_size("c")
    other = lax.ppermute(own, "c", [(i, cores - 1 - i) for i in range(cores)])

    merged, left_copies = pl.pallas_call(
        merge_kernel,
        out_shape=[
            jax.ShapeDtypeStruct((features, width), F32),
            jax.ShapeDtypeStruct((across, rank, features), BF16),
        ],
        compiler_params=params(),
        name="merge",
    )(kept_features, own, other, error_old, initial_q.T)

    left_copies = add_copies(to_all(left_copies, "z"), lax.axis_size("y"), BF16)
    left_copies = to_all(left_copies, "y")

    left, q_pieces = pl.pallas_call(
        functools.partial(project_kernel, replicas),
        out_shape=[
            jax.ShapeDtypeStruct((rank, features), F32),
            jax.ShapeDtypeStruct((crowd, rank + lines, lanes), F32),
        ],
        compiler_params=params(),
        name="project",
    )(left_copies, merged)

    q_copies, gram = pl.pallas_call(
        functools.partial(add_blocks_kernel, rank),
        out_shape=[
            jax.ShapeDtypeStruct((across, rank, lanes), F32),
            jax.ShapeDtypeStruct((lines, lanes), F32),
        ],
        compiler_params=params(),
        name="add_blocks",
    )(to_all(q_pieces, TENSOR))
    q_copies = add_copies(to_all(q_copies, "z"), lax.axis_size("y"), F32)
    q_copies = add_copies(to_all(q_copies, "y"), crowd, F32)
    q_pieces = to_all(q_copies, TENSOR)

    rows = features // 4
    error_new, own_q = pl.pallas_call(
        functools.partial(finish_kernel, replicas),
        out_specs=[in_hbm(), whole((rank, lanes))],
        out_shape=[
            jax.ShapeDtypeStruct((features, width), BF16),
            jax.ShapeDtypeStruct((rank, lanes), F32),
        ],
        scratch_shapes=[
            pltpu.VMEM((rank, width), F32),
            pltpu.VMEM((4, rows, width), BF16),
            pltpu.SemaphoreType.DMA((4,)),
        ],
        compiler_params=params(),
        name="finish",
    )(q_pieces, gram, left, merged)
    return error_new, own_q.T


def solution(mesh, sizes=(8, 8, 4, 2)):
    finer = Mesh(mesh.devices.reshape(sizes), ("y", "z", "x", "c"))
    everyone = ("y", "z", "x", "c")
    in_specs = (P(DP, TENSOR), P(DP, TENSOR), P(everyone, None), P(), P())
    out_specs = (P(everyone, None), P(TENSOR, None))
    return jax.shard_map(
        body, mesh=finer, in_specs=in_specs, out_specs=out_specs, check_vma=False
    )
```

profile of v0, /device:TPU:1, one launch (start us, length us, event | category | flops | bytes accessed | tf_op | source)
XLA Modules:
  0.0 121.4 jit_solution(12474568385121030887)
XLA Ops:
  0.6 0.7 reshape.7.pause_ref
  1.3 0.0 copy-start.1
  1.3 1.0 copy-done.1
  2.3 1.2 compact_cotangents.1
  3.5 0.0 copy-start.3
  3.5 14.4 %all_to_all.35.own_ref = bf16[4,960,128]{2,1,0:T(8,128)(2,1)S(1)} all-to-all(bf16[4,960,128]{2,1,0:T(8,128)(2,1)S(1)} %compact_cotangents.1), channel_id=1, replica_groups=mesh['y'=8,'z'=8,'x'=4,'c'=2] {'x'}, dimensions={0} | all-to-all | bytes 1966080 | tf_op jit(solution)/shard_map/all_to_all | solution.py:214
  17.8 0.0 copy-start
  17.8 0.0 copy-start.2
  17.8 7.8 %collective-permute-start = (bf16[4,960,128]{2,1,0:T(8,128)(2,1)S(1)}, bf16[4,960,128]{2,1,0:T(8,128)(2,1)S(1)}, u32[]{:S(2)}, u32[]{:S(2)}) collective-permute-start(bf16[4,960,128]{2,1,0:T(8,128)(2,1)S(1)} %all_to_all.35.own_ref), channel_id=1, source_target_pairs={{0,1},{1,0},{2,3},{3,2},{4,5},{5,4},{6,7},{7,6},{8,9},{9,8},{10,11... | collective-permute-start | bytes 2949128 | tf_op jit(solution)/shard_map/ppermute | solution.py:258
  25.6 0.0 copy-done.3
  25.7 2.6 %compact_features.1.feat_ref = bf16[640,1024]{1,0:T(8,128)(2,1)S(1)} custom-call(s32[1,320]{1,0:T(1,128)S(1)} %reshape.7.pause_ref, bf16[1280,640]{1,0:T(8,128)(2,1)S(1)} %copy-done.3), custom_call_target="tpu_custom_call" | custom-call | flops 1572864000 | bytes 3276800 | tf_op jit(solution)/shard_map/compact_features/pallas_call | solution.py:246
  28.2 0.0 collective-permute-done.other_ref
  28.2 0.0 copy-done
  28.2 0.0 copy-done.2
  28.3 2.6 %merge.1 = (f32[640,1024]{1,0:T(8,128)S(1)}, bf16[8,32,640]{2,1,0:T(8,128)(2,1)S(1)}) custom-call(bf16[640,1024]{1,0:T(8,128)(2,1)S(1)} %compact_features.1.feat_ref, bf16[4,960,128]{2,1,0:T(8,128)(2,1)S(1)} %all_to_all.35.own_ref, bf16[4,960,128]{2,1,0:T(8,128)(2,1)S(1)} %collective-permute-done.other_ref, bf16[640,1024]{1,0:T(8,128)(2,1)S(1)} %copy-done, ...), custom_call_target="tpu_custom_call" | custom-call | tf_op jit(solution)/shard_map/merge/pallas_call | solution.py:260
  30.9 23.6 %all_to_all.36.in_ref = bf16[8,32,640]{2,1,0:T(8,128)(2,1)S(1)} all-to-all(bf16[8,32,640]{2,1,0:T(8,128)(2,1)S(1)} %get-tuple-element.10), channel_id=1, replica_groups=mesh['y'=8,'z'=8,'x'=4,'c'=2] {'z'}, dimensions={0} | all-to-all | bytes 655360 | tf_op jit(solution)/shard_map/all_to_all | solution.py:214
  54.5 0.1 add_copies.3
  54.5 19.3 %all_to_all.37.in_ref = bf16[8,32,640]{2,1,0:T(8,128)(2,1)S(1)} all-to-all(bf16[8,32,640]{2,1,0:T(8,128)(2,1)S(1)} %add_copies.3), channel_id=1, replica_groups=mesh['y'=8,'z'=8,'x'=4,'c'=2] {'y'}, dimensions={0} | all-to-all | bytes 655360 | tf_op jit(solution)/shard_map/all_to_all | solution.py:214
  73.8 0.6 project.1
  74.4 9.5 %all_to_all.38.in_ref = f32[8,40,128]{2,1,0:T(8,128)S(1)} all-to-all(f32[8,40,128]{2,1,0:T(8,128)S(1)} %get-tuple-element.12), channel_id=1, replica_groups=mesh['y'=8,'z'=8,'x'=4,'c'=2] {'x','c'}, dimensions={0} | all-to-all | bytes 327680 | tf_op jit(solution)/shard_map/all_to_all | solution.py:214
  84.0 10.1 %all_to_all.39.in_ref = f32[8,32,128]{2,1,0:T(8,128)S(1)} all-to-all(f32[8,32,128]{2,1,0:T(8,128)S(1)} %get-tuple-element.13), channel_id=1, replica_groups=mesh['y'=8,'z'=8,'x'=4,'c'=2] {'z'}, dimensions={0} | all-to-all | bytes 262144 | tf_op jit(solution)/shard_map/all_to_all | solution.py:214
  94.1 10.4 %all_to_all.40.in_ref = f32[8,32,128]{2,1,0:T(8,128)S(1)} all-to-all(f32[8,32,128]{2,1,0:T(8,128)S(1)} %add_copies.4), channel_id=1, replica_groups=mesh['y'=8,'z'=8,'x'=4,'c'=2] {'y'}, dimensions={0} | all-to-all | bytes 262144 | tf_op jit(solution)/shard_map/all_to_all | solution.py:214
  104.5 10.9 %all_to_all.41.in_ref = f32[8,32,128]{2,1,0:T(8,128)S(1)} all-to-all(f32[8,32,128]{2,1,0:T(8,128)S(1)} %add_copies.5), channel_id=1, replica_groups=mesh['y'=8,'z'=8,'x'=4,'c'=2] {'x','c'}, dimensions={0} | all-to-all | bytes 262144 | tf_op jit(solution)/shard_map/all_to_all | solution.py:214
  115.5 5.9 %finish.1 = (bf16[640,1024]{1,0:T(8,128)(2,1)}, f32[32,128]{1,0:T(8,128)}) custom-call(f32[8,32,128]{2,1,0:T(8,128)S(1)} %all_to_all.41.in_ref, f32[8,128]{1,0:T(8,128)S(1)} %get-tuple-element.14.gram_ref, f32[32,640]{1,0:T(8,128)S(1)} %get-tuple-element.15.left_ref, f32[640,1024]{1,0:T(8,128)S(1)} %get-tuple-element.11.merged_ref), custom_call_target="tpu_custom_call" | custom-call | tf_op jit(solution)/shard_map/finish/pallas_call | solution.py:297
  (3 shorter events, 0.1 us)
Async XLA Ops:
  1.3 1.0 copy-start.1
  3.5 22.2 %copy-start.3 = (bf16[1280,640]{1,0:T(8,128)(2,1)S(1)}, bf16[1280,640]{1,0:T(8,128)(2,1)}, u32[]{:S(2)}) copy-start(bf16[1280,640]{1,0:T(8,128)(2,1)} %act_ref.1) | copy-start | bytes 4915204
  17.8 10.4 %copy-start = (bf16[640,1024]{1,0:T(8,128)(2,1)S(1)}, bf16[640,1024]{1,0:T(8,128)(2,1)}, u32[]{:S(2)}) copy-start(bf16[640,1024]{1,0:T(8,128)(2,1)} %err_ref.1) | copy-start | bytes 3932164
  17.8 10.4 %copy-start.2 = (f32[1024,32]{0,1:T(8,128)S(1)}, f32[1024,32]{0,1:T(8,128)}, u32[]{:S(2)}) copy-start(f32[1024,32]{0,1:T(8,128)} %param.9) | copy-start | bytes 393220
  17.8 10.4 %collective-permute-start = (bf16[4,960,128]{2,1,0:T(8,128)(2,1)S(1)}, bf16[4,960,128]{2,1,0:T(8,128)(2,1)S(1)}, u32[]{:S(2)}, u32[]{:S(2)}) collective-permute-start(bf16[4,960,128]{2,1,0:T(8,128)(2,1)S(1)} %all_to_all.35.own_ref), channel_id=1, source_target_pairs={{0,1},{1,0},{2,3},{3,2},{4,5},{5,4},{6,7},{7,6},{8,9},{9,8},{10,11... | collective-permute-start | bytes 2949128 | tf_op jit(solution)/shard_map/ppermute | solution.py:258
where the time goes:
time: 122 us; the launch traced here: 121 us
  blocking collectives  98.2 us (80%)
  Pallas kernels  12.9 us (11%)
  starting transfers between devices  7.79 us (6%)
  local copies, waits for them, and re-layouts  1.67 us (1%)
    all_to_all x7, blocking collectives, to_all(): return lax.all_to_all(pieces, axes, split_axis=0, concat_axis=0, tiled=True)  98.2 us
    ppermute x1, starting transfers between devices, body(): other = lax.ppermute(own, 'c', [(i, cores - 1 - i) for i in range(cores)])  7.79 us
    pallas_call x1, Pallas kernels, body(): pl.pallas_call(functools.partial(finish_kernel, replicas), out_specs=[in_...  5.88 us
    pallas_call x1, Pallas kernels, body(): pl.pallas_call(merge_kernel, out_shape=[jax.ShapeDtypeStruct((features, w...  2.59 us
    pallas_call x1, Pallas kernels, body(): pl.pallas_call(functools.partial(compact_features_kernel, kept_count), ou...  2.56 us
  transfers between devices with their start and end apart: 1, of which 0 were waited for; matrix products, arithmetic and copies ran while one was open for 0% of the time, Pallas kernels for 2%

commit v1 on v0

--- a/solution.py
+++ b/solution.py
@@ -12,6 +12,7 @@
 TENSOR = ("x", "c")
 CHUNK = 256
 LANES = 128
+BLOCKS = 5
 MIB = 1024 * 1024
 F32 = jnp.float32
 BF16 = jnp.bfloat16
@@ -32,31 +33,41 @@
     return high, (x - high.astype(F32)).astype(BF16)
 
 
-def selection(pauses, row_count, kept_count):
-    count = pauses.shape[1]
+def kept_ranks(pauses, row_count):
+    count = pauses.shape[0]
     row = lax.broadcasted_iota(jnp.int32, (count, count), 0)
     col = lax.broadcasted_iota(jnp.int32, (count, count), 1)
-    column = jnp.sum(
-        jnp.where(row == col, pauses.astype(F32), 0.0), axis=1, keepdims=True
-    )
+    wide = pauses.astype(F32).reshape(1, count)
+    column = jnp.sum(jnp.where(row == col, wide, 0.0), axis=1, keepdims=True)
     spot = lax.broadcasted_iota(jnp.int32, (1, row_count), 1).astype(F32)
     before = jnp.sum(jnp.where(column < spot, 1.0, 0.0), axis=0, keepdims=True)
     struck = jnp.sum(jnp.where(column == spot, 1.0, 0.0), axis=0, keepdims=True)
-    target = jnp.where(struck > 0.0, -1.0, spot - before)
-    rank = lax.broadcasted_iota(jnp.int32, (kept_count, row_count), 0).astype(F32)
-    return jnp.where(rank == target, 1.0, 0.0).astype(BF16)
+    return jnp.where(struck > 0.0, -1.0, spot - before)
+
+
+def kept_rows(pauses, values_ref, kept_count):
+    row_count = values_ref.shape[0]
+    ranks = kept_ranks(pauses, row_count)
+    size = kept_count // BLOCKS
+    window = size + row_count - kept_count
+    blocks = []
+    for block in range(BLOCKS):
+        start = block * size
+        here = ranks if start == 0 else pltpu.roll(ranks, row_count - start, 1)
+        rank = lax.broadcasted_iota(jnp.int32, (size, window), 0) + start
+        pick = jnp.where(rank.astype(F32) == here[:, :window], 1.0, 0.0).astype(BF16)
+        blocks.append(dot(pick, values_ref[start : start + window], ((1,), (0,))))
+    return jnp.concatenate(blocks, axis=0)
 
 
 def compact_cotangents_kernel(pause_ref, cot_ref, out_ref):
-    pick = selection(pause_ref[...], cot_ref.shape[0], out_ref.shape[1])
-    kept = dot(pick, cot_ref[...], ((1,), (0,))).astype(BF16)
+    kept = kept_rows(pause_ref[...], cot_ref, out_ref.shape[1]).astype(BF16)
     for copy in range(out_ref.shape[0]):
         out_ref[copy] = kept
 
 
 def compact_features_kernel(kept_count, pause_ref, act_ref, out_ref):
-    pick = selection(pause_ref[...], act_ref.shape[0], kept_count)
-    kept = dot(pick, act_ref[...], ((1,), (0,)))
+    kept = kept_rows(pause_ref[...], act_ref, kept_count)
     spare = jnp.zeros((out_ref.shape[1] - kept_count, kept.shape[1]), F32)
     out_ref[...] = jnp.concatenate([kept, spare], axis=0).T.astype(BF16)
 
@@ -145,7 +156,7 @@
     for copy in range(1, in_ref.shape[0]):
         total += in_ref[copy]
     for copy in range(out_ref.shape[0]):
-        out_ref[copy] = total[:rank]
+        out_ref[copy] = total[:rank].astype(out_ref.dtype)
     gram_ref[...] = total[rank:]
 
 
@@ -174,15 +185,16 @@
     rank, width = q_ref.shape
     inverse = inverse_factor(unpack(gram_ref[...], rank))
     raw = jnp.concatenate([in_ref[piece] for piece in range(in_ref.shape[0])], axis=1)
-    q_new = dot(inverse, raw / replicas, ((1,), (0,)), lax.Precision.HIGHEST)
-    basis = dot(inverse, left_ref[...], ((1,), (0,)), lax.Precision.HIGHEST)
-    q_ref[...] = q_new
+    raw = raw / replicas
+    q_ref[...] = raw
     lanes = own_ref.shape[1]
     place = lax.axis_index("x") * lax.axis_size("c") + lax.axis_index("c")
-    own_ref[...] = q_ref[:, pl.ds(pl.multiple_of(place * lanes, lanes), lanes)]
-    high, low = split(q_new)
+    own = q_ref[:, pl.ds(pl.multiple_of(place * lanes, lanes), lanes)]
+    own_ref[...] = dot(inverse, own, ((1,), (0,)), lax.Precision.HIGHEST)
+    square = dot(inverse.T, inverse, ((1,), (0,)), lax.Precision.HIGHEST)
+    high, low = split(dot(square, raw, ((1,), (0,)), lax.Precision.HIGHEST))
     stack = jnp.concatenate([high, high, low, jnp.zeros_like(high)], axis=0)
-    high, low = split(basis)
+    high, low = split(left_ref[...])
     high = high.astype(F32)
     low = low.astype(F32)
     turned = jnp.concatenate([high, low, high, jnp.zeros_like(high)], axis=0).T.astype(BF16)
@@ -234,7 +246,7 @@
     crowd = lax.axis_size(TENSOR)
     chunks = width // CHUNK
     lines = rank * rank // LANES
-    pauses = pause_positions.reshape(1, -1)
+    pauses = pause_positions
 
     cot_copies = pl.pallas_call(
         compact_cotangents_kernel,
@@ -283,7 +295,7 @@
     q_copies, gram = pl.pallas_call(
         functools.partial(add_blocks_kernel, rank),
         out_shape=[
-            jax.ShapeDtypeStruct((across, rank, lanes), F32),
+            jax.ShapeDtypeStruct((across, rank, lanes), BF16),
             jax.ShapeDtypeStruct((lines, lanes), F32),
         ],
         compiler_params=params(),
@@ -293,7 +305,7 @@
     q_copies = add_copies(to_all(q_copies, "y"), crowd, F32)
     q_pieces = to_all(q_copies, TENSOR)
 
-    rows = features // 4
+    parts = features // LANES
     error_new, own_q = pl.pallas_call(
         functools.partial(finish_kernel, replicas),
         out_specs=[in_hbm(), whole((rank, lanes))],
@@ -303,8 +315,8 @@
         ],
         scratch_shapes=[
             pltpu.VMEM((rank, width), F32),
-            pltpu.VMEM((4, rows, width), BF16),
-            pltpu.SemaphoreType.DMA((4,)),
+            pltpu.VMEM((parts, LANES, width), BF16),
+            pltpu.SemaphoreType.DMA((parts,)),
         ],
         compiler_params=params(),
         name="finish",

time: 122 us -> 119 us (0.975)
  blocking collectives: 98.2 us -> 96.5 us
  Pallas kernels: 12.9 us -> 11.5 us
    all_to_all x7, blocking collectives: 98.2 us -> 96.5 us  [to_all(): return lax.all_to_all(pieces, axes, split_axis=0, concat_axis=0, tiled=True)]
  transfers between devices with their start and end apart: 1 -> 1, of which waited for: 0 -> 1; matrix products, arithmetic and copies ran while one was open for 0% -> 0% of each run, Pallas kernels for 2% -> 1%
where the time goes in v1:
time: 119 us
  blocking collectives  96.5 us (81%)
  Pallas kernels  11.5 us (10%)
  starting transfers between devices  7.79 us (7%)
  local copies, waits for them, and re-layouts  1.66 us (1%)
    all_to_all x7, blocking collectives, to_all(): return lax.all_to_all(pieces, axes, split_axis=0, concat_axis=0, tiled=True)  96.5 us
    ppermute x1, starting transfers between devices, body(): other = lax.ppermute(own, 'c', [(i, cores - 1 - i) for i in range(cores)])  7.79 us
    pallas_call x1, Pallas kernels, body(): pl.pallas_call(functools.partial(finish_kernel, replicas), out_specs=[in_...  5.95 us
    pallas_call x1, Pallas kernels, body(): pl.pallas_call(merge_kernel, out_shape=[jax.ShapeDtypeStruct((features, w...  2.59 us
  transfers between devices with their start and end apart: 1, of which 1 were waited for; matrix products, arithmetic and copies ran while one was open for 0% of the time, Pallas kernels for 1%

profile of v1, /device:TPU:1, one launch (start us, length us, event | category | flops | bytes accessed | tf_op | source)
XLA Modules:
  0.0 118.8 jit_solution(2090192889427467247)
XLA Ops:
  0.6 0.0 copy-start.1
  0.6 1.0 copy-done.1
  1.6 0.0 copy-start.3
  1.6 0.7 copy-done.3
  2.3 0.8 compact_cotangents.1
  3.0 0.0 copy-start.4
  3.1 14.4 %all_to_all.35.own_ref = bf16[4,960,128]{2,1,0:T(8,128)(2,1)S(1)} all-to-all(bf16[4,960,128]{2,1,0:T(8,128)(2,1)S(1)} %compact_cotangents.1), channel_id=1, replica_groups=mesh['y'=8,'z'=8,'x'=4,'c'=2] {'x'}, dimensions={0} | all-to-all | bytes 1966080 | tf_op jit(solution)/shard_map/all_to_all | solution.py:226
  17.4 0.0 copy-start
  17.4 0.0 copy-start.2
  17.4 7.8 %collective-permute-start = (bf16[4,960,128]{2,1,0:T(8,128)(2,1)S(1)}, bf16[4,960,128]{2,1,0:T(8,128)(2,1)S(1)}, u32[]{:S(2)}, u32[]{:S(2)}) collective-permute-start(bf16[4,960,128]{2,1,0:T(8,128)(2,1)S(1)} %all_to_all.35.own_ref), channel_id=1, source_target_pairs={{0,1},{1,0},{2,3},{3,2},{4,5},{5,4},{6,7},{7,6},{8,9},{9,8},{10,11... | collective-permute-start | bytes 2949128 | tf_op jit(solution)/shard_map/ppermute | solution.py:270
  25.2 0.0 copy-done.4
  25.2 1.4 %compact_features.1.feat_ref = bf16[640,1024]{1,0:T(8,128)(2,1)S(1)} custom-call(s32[320]{0:T(512)S(1)} %copy-done.3, bf16[1280,640]{1,0:T(8,128)(2,1)S(1)} %copy-done.4), custom_call_target="tpu_custom_call" | custom-call | flops 1572864000 | bytes 3276800 | tf_op jit(solution)/shard_map/compact_features/pallas_call | solution.py:258
  26.7 0.7 collective-permute-done.other_ref
  27.4 0.0 copy-done
  27.4 0.0 copy-done.2
  27.4 2.6 %merge.1 = (f32[640,1024]{1,0:T(8,128)S(1)}, bf16[8,32,640]{2,1,0:T(8,128)(2,1)S(1)}) custom-call(bf16[640,1024]{1,0:T(8,128)(2,1)S(1)} %compact_features.1.feat_ref, bf16[4,960,128]{2,1,0:T(8,128)(2,1)S(1)} %all_to_all.35.own_ref, bf16[4,960,128]{2,1,0:T(8,128)(2,1)S(1)} %collective-permute-done.other_ref, bf16[640,1024]{1,0:T(8,128)(2,1)S(1)} %copy-done, ...), custom_call_target="tpu_custom_call" | custom-call | tf_op jit(solution)/shard_map/merge/pallas_call | solution.py:272
  30.0 22.6 %all_to_all.36.in_ref = bf16[8,32,640]{2,1,0:T(8,128)(2,1)S(1)} all-to-all(bf16[8,32,640]{2,1,0:T(8,128)(2,1)S(1)} %get-tuple-element.10), channel_id=1, replica_groups=mesh['y'=8,'z'=8,'x'=4,'c'=2] {'z'}, dimensions={0} | all-to-all | bytes 655360 | tf_op jit(solution)/shard_map/all_to_all | solution.py:226
  52.6 0.1 add_copies.3
  52.7 17.4 %all_to_all.37.in_ref = bf16[8,32,640]{2,1,0:T(8,128)(2,1)S(1)} all-to-all(bf16[8,32,640]{2,1,0:T(8,128)(2,1)S(1)} %add_copies.3), channel_id=1, replica_groups=mesh['y'=8,'z'=8,'x'=4,'c'=2] {'y'}, dimensions={0} | all-to-all | bytes 655360 | tf_op jit(solution)/shard_map/all_to_all | solution.py:226
  70.1 0.6 project.1
  70.7 11.4 %all_to_all.38.in_ref = f32[8,40,128]{2,1,0:T(8,128)S(1)} all-to-all(f32[8,40,128]{2,1,0:T(8,128)S(1)} %get-tuple-element.12), channel_id=1, replica_groups=mesh['y'=8,'z'=8,'x'=4,'c'=2] {'x','c'}, dimensions={0} | all-to-all | bytes 327680 | tf_op jit(solution)/shard_map/all_to_all | solution.py:226
  82.1 9.7 %all_to_all.39.in_ref = bf16[8,32,128]{2,1,0:T(8,128)(2,1)S(1)} all-to-all(bf16[8,32,128]{2,1,0:T(8,128)(2,1)S(1)} %get-tuple-element.13), channel_id=1, replica_groups=mesh['y'=8,'z'=8,'x'=4,'c'=2] {'z'}, dimensions={0} | all-to-all | bytes 131072 | tf_op jit(solution)/shard_map/all_to_all | solution.py:226
  91.8 10.4 %all_to_all.40.in_ref = f32[8,32,128]{2,1,0:T(8,128)S(1)} all-to-all(f32[8,32,128]{2,1,0:T(8,128)S(1)} %add_copies.4), channel_id=1, replica_groups=mesh['y'=8,'z'=8,'x'=4,'c'=2] {'y'}, dimensions={0} | all-to-all | bytes 262144 | tf_op jit(solution)/shard_map/all_to_all | solution.py:226
  102.2 10.6 %all_to_all.41.in_ref = f32[8,32,128]{2,1,0:T(8,128)S(1)} all-to-all(f32[8,32,128]{2,1,0:T(8,128)S(1)} %add_copies.5), channel_id=1, replica_groups=mesh['y'=8,'z'=8,'x'=4,'c'=2] {'x','c'}, dimensions={0} | all-to-all | bytes 262144 | tf_op jit(solution)/shard_map/all_to_all | solution.py:226
  112.9 5.9 %finish.1 = (bf16[640,1024]{1,0:T(8,128)(2,1)}, f32[32,128]{1,0:T(8,128)}) custom-call(f32[8,32,128]{2,1,0:T(8,128)S(1)} %all_to_all.41.in_ref, f32[8,128]{1,0:T(8,128)S(1)} %get-tuple-element.14.gram_ref, f32[32,640]{1,0:T(8,128)S(1)} %get-tuple-element.15.left_ref, f32[640,1024]{1,0:T(8,128)S(1)} %get-tuple-element.11.merged_ref), custom_call_target="tpu_custom_call" | custom-call | tf_op jit(solution)/shard_map/finish/pallas_call | solution.py:309
  (3 shorter events, 0.1 us)
Async XLA Ops:
  0.6 1.0 copy-start.1
  1.6 0.7 copy-start.3
  3.0 22.2 %copy-start.4 = (bf16[1280,640]{1,0:T(8,128)(2,1)S(1)}, bf16[1280,640]{1,0:T(8,128)(2,1)}, u32[]{:S(2)}) copy-start(bf16[1280,640]{1,0:T(8,128)(2,1)} %act_ref.1) | copy-start | bytes 4915204
  17.4 10.0 %copy-start = (bf16[640,1024]{1,0:T(8,128)(2,1)S(1)}, bf16[640,1024]{1,0:T(8,128)(2,1)}, u32[]{:S(2)}) copy-start(bf16[640,1024]{1,0:T(8,128)(2,1)} %err_ref.1) | copy-start | bytes 3932164
  17.4 10.0 %copy-start.2 = (f32[1024,32]{0,1:T(8,128)S(1)}, f32[1024,32]{0,1:T(8,128)}, u32[]{:S(2)}) copy-start(f32[1024,32]{0,1:T(8,128)} %param.9) | copy-start | bytes 393220
  17.4 10.0 %collective-permute-start = (bf16[4,960,128]{2,1,0:T(8,128)(2,1)S(1)}, bf16[4,960,128]{2,1,0:T(8,128)(2,1)S(1)}, u32[]{:S(2)}, u32[]{:S(2)}) collective-permute-start(bf16[4,960,128]{2,1,0:T(8,128)(2,1)S(1)} %all_to_all.35.own_ref), channel_id=1, source_target_pairs={{0,1},{1,0},{2,3},{3,2},{4,5},{5,4},{6,7},{7,6},{8,9},{9,8},{10,11... | collective-permute-start | bytes 2949128 | tf_op jit(solution)/shard_map/ppermute | solution.py:270

commit v2 on v1

--- a/solution.py
+++ b/solution.py
@@ -164,21 +164,26 @@
     rank = gram.shape[0]
     row = lax.broadcasted_iota(jnp.int32, (rank, rank), 0)
     col = lax.broadcasted_iota(jnp.int32, (rank, rank), 1)
-    table = jnp.concatenate([gram, jnp.where(row == col, 1.0, 0.0)], axis=1)
-    line = lax.broadcasted_iota(jnp.int32, (rank, 1), 0)
+    spare = jnp.zeros((rank, LANES - 2 * rank), F32)
+    table = jnp.concatenate([jnp.where(row == col, 1.0, 0.0), gram, spare], axis=1)
+    line = lax.broadcasted_iota(jnp.int32, (rank, LANES), 0)
+    pivots = jnp.ones((rank, LANES), F32)
     for k in range(0, rank, 2):
-        column, second = table[:, k : k + 1], table[:, k + 1 : k + 2]
-        inverse = 1.0 / column[k : k + 1]
+        at = rank + k
+        column = jnp.broadcast_to(table[:, at : at + 1], (rank, LANES))
+        second = jnp.broadcast_to(table[:, at + 1 : at + 2], (rank, LANES))
+        pivot = column[k : k + 1]
+        inverse = 1.0 / pivot
         slope = column[k + 1 : k + 2] * inverse
-        pivot = second[k + 1 : k + 2] - slope * second[k : k + 1]
-        top = table[k : k + 1, :]
-        bottom = table[k + 1 : k + 2, :] - slope * top
+        after = second[k + 1 : k + 2] - slope * second[k : k + 1]
+        top = table[k : k + 1]
+        bottom = table[k + 1 : k + 2] - slope * top
         below = line > k + 1
         upper = jnp.where(below, column * inverse, 0.0)
-        lower = jnp.where(below, (second - slope * column) / pivot, 0.0)
+        lower = jnp.where(below, second - slope * column, 0.0) * (1.0 / after)
         table = jnp.where(line == k + 1, bottom, table - upper * top - lower * bottom)
-    diagonal = jnp.sum(jnp.where(row == col, table[:, :rank], 0.0), axis=1, keepdims=True)
-    return table[:, rank:] / jnp.sqrt(diagonal)
+        pivots = jnp.where(line == k, pivot, jnp.where(line == k + 1, after, pivots))
+    return (table / jnp.sqrt(pivots))[:, :rank]
 
 
 def finish_kernel(replicas, in_ref, gram_ref, left_ref, merged_ref, err_hbm, own_ref, q_ref, err_ref, sems):
@@ -222,6 +227,20 @@
     return pl.BlockSpec(shape, lambda *_: (0,) * len(shape))
 
 
+def to_column(pieces, turn):
+    axes = ("y", "z", "c")
+    ny, nz, nc = (lax.axis_size(axis) for axis in axes)
+    groups = []
+    for core in range(nc):
+        if (core + turn) % 2 == 0:
+            groups += [[(y * nz + z) * nc + core for z in range(nz)] for y in range(ny)]
+        else:
+            groups += [[(y * nz + z) * nc + core for y in range(ny)] for z in range(nz)]
+    return lax.all_to_all(
+        pieces, axes, split_axis=0, concat_axis=0, tiled=True, axis_index_groups=groups
+    )
+
+
 def to_all(pieces, axes):
     return lax.all_to_all(pieces, axes, split_axis=0, concat_axis=0, tiled=True)
 
@@ -279,8 +298,8 @@
         name="merge",
     )(kept_features, own, other, error_old, initial_q.T)
 
-    left_copies = add_copies(to_all(left_copies, "z"), lax.axis_size("y"), BF16)
-    left_copies = to_all(left_copies, "y")
+    left_copies = add_copies(to_column(left_copies, 0), lax.axis_size("y"), BF16)
+    left_copies = to_column(left_copies, 1)
 
     left, q_pieces = pl.pallas_call(
         functools.partial(project_kernel, replicas),
@@ -301,8 +320,8 @@
         compiler_params=params(),
         name="add_blocks",
     )(to_all(q_pieces, TENSOR))
-    q_copies = add_copies(to_all(q_copies, "z"), lax.axis_size("y"), F32)
-    q_copies = add_copies(to_all(q_copies, "y"), crowd, F32)
+    q_copies = add_copies(to_column(q_copies, 0), lax.axis_size("y"), F32)
+    q_copies = add_copies(to_column(q_copies, 1), crowd, F32)
     q_pieces = to_all(q_copies, TENSOR)
 
     parts = features // LANES

time: 119 us -> 114 us (0.958)
  blocking collectives: 96.5 us -> 92.8 us
  Pallas kernels: 11.5 us -> 9.48 us
    all_to_all x7 -> x3, blocking collectives: 96.5 us -> 36.4 us  [to_all(): return lax.all_to_all(pieces, axes, split_axis=0, concat_axis=0, tiled=True)]
    all_to_all x0 -> x4, blocking collectives: none -> 56.4 us  [to_column(): lax.all_to_all(pieces, axes, split_axis=0, concat_axis=0, tiled=True, axi...]
    pallas_call x1, Pallas kernels: 5.95 us -> 3.98 us  [body(): pl.pallas_call(functools.partial(finish_kernel, replicas), out_specs=[in_...]
where the time goes in v2:
time: 114 us; the launch traced here: 113 us
  blocking collectives  92.8 us (81%)
  Pallas kernels  9.48 us (8%)
  starting transfers between devices  7.79 us (7%)
  local copies, waits for them, and re-layouts  1.66 us (1%)
    all_to_all x4, blocking collectives, to_column(): lax.all_to_all(pieces, axes, split_axis=0, concat_axis=0, tiled=True, axi...  56.4 us
    all_to_all x3, blocking collectives, to_all(): return lax.all_to_all(pieces, axes, split_axis=0, concat_axis=0, tiled=True)  36.4 us
    ppermute x1, starting transfers between devices, body(): other = lax.ppermute(own, 'c', [(i, cores - 1 - i) for i in range(cores)])  7.79 us
    pallas_call x1, Pallas kernels, body(): pl.pallas_call(functools.partial(finish_kernel, replicas), out_specs=[in_...  3.98 us
    pallas_call x1, Pallas kernels, body(): pl.pallas_call(merge_kernel, out_shape=[jax.ShapeDtypeStruct((features, w...  2.59 us
  transfers between devices with their start and end apart: 1, of which 1 were waited for; matrix products, arithmetic and copies ran while one was open for 0% of the time, Pallas kernels for 1%

profile of v2, /device:TPU:1, one launch (start us, length us, event | category | flops | bytes accessed | tf_op | source)
XLA Modules:
  0.0 113.2 jit_solution(117711183674114856)
XLA Ops:
  0.6 0.0 copy-start.1
  0.6 1.0 copy-done.1
  1.6 0.0 copy-start.3
  1.6 0.7 copy-done.3
  2.3 0.8 compact_cotangents.1
  3.0 0.0 copy-start.4
  3.1 14.4 %all_to_all.35.own_ref = bf16[4,960,128]{2,1,0:T(8,128)(2,1)S(1)} all-to-all(bf16[4,960,128]{2,1,0:T(8,128)(2,1)S(1)} %compact_cotangents.1), channel_id=1, replica_groups=mesh['y'=8,'z'=8,'x'=4,'c'=2] {'x'}, dimensions={0} | all-to-all | bytes 1966080 | tf_op jit(solution)/shard_map/all_to_all | solution.py:245
  17.4 0.0 copy-start
  17.4 0.0 copy-start.2
  17.4 7.8 %collective-permute-start = (bf16[4,960,128]{2,1,0:T(8,128)(2,1)S(1)}, bf16[4,960,128]{2,1,0:T(8,128)(2,1)S(1)}, u32[]{:S(2)}, u32[]{:S(2)}) collective-permute-start(bf16[4,960,128]{2,1,0:T(8,128)(2,1)S(1)} %all_to_all.35.own_ref), channel_id=1, source_target_pairs={{0,1},{1,0},{2,3},{3,2},{4,5},{5,4},{6,7},{7,6},{8,9},{9,8},{10,11... | collective-permute-start | bytes 2949128 | tf_op jit(solution)/shard_map/ppermute | solution.py:289
  25.2 0.0 copy-done.4
  25.2 1.4 %compact_features.1.feat_ref = bf16[640,1024]{1,0:T(8,128)(2,1)S(1)} custom-call(s32[320]{0:T(512)S(1)} %copy-done.3, bf16[1280,640]{1,0:T(8,128)(2,1)S(1)} %copy-done.4), custom_call_target="tpu_custom_call" | custom-call | flops 1572864000 | bytes 3276800 | tf_op jit(solution)/shard_map/compact_features/pallas_call | solution.py:277
  26.7 0.7 collective-permute-done.other_ref
  27.4 0.0 copy-done
  27.4 0.0 copy-done.2
  27.4 2.6 %merge.1 = (f32[640,1024]{1,0:T(8,128)S(1)}, bf16[8,32,640]{2,1,0:T(8,128)(2,1)S(1)}) custom-call(bf16[640,1024]{1,0:T(8,128)(2,1)S(1)} %compact_features.1.feat_ref, bf16[4,960,128]{2,1,0:T(8,128)(2,1)S(1)} %all_to_all.35.own_ref, bf16[4,960,128]{2,1,0:T(8,128)(2,1)S(1)} %collective-permute-done.other_ref, bf16[640,1024]{1,0:T(8,128)(2,1)S(1)} %copy-done, ...), custom_call_target="tpu_custom_call" | custom-call | tf_op jit(solution)/shard_map/merge/pallas_call | solution.py:291
  30.0 16.7 %all_to_all.36.in_ref = bf16[8,32,640]{2,1,0:T(8,128)(2,1)S(1)} all-to-all(bf16[8,32,640]{2,1,0:T(8,128)(2,1)S(1)} %get-tuple-element.10), channel_id=1, replica_groups={{0,8,16,24,32,40,48,56},{64,72,80,88,96,104,112,120},{128,136,144,152,1..., dimensions={0} | all-to-all | bytes 655360 | tf_op jit(solution)/shard_map/all_to_all | solution.py:239
  46.6 0.1 add_copies.3
  46.7 19.9 %all_to_all.37.in_ref = bf16[8,32,640]{2,1,0:T(8,128)(2,1)S(1)} all-to-all(bf16[8,32,640]{2,1,0:T(8,128)(2,1)S(1)} %add_copies.3), channel_id=1, replica_groups={{0,64,128,192,256,320,384,448},{8,72,136,200,264,328,392,456},{16,80,14..., dimensions={0} | all-to-all | bytes 655360 | tf_op jit(solution)/shard_map/all_to_all | solution.py:239
  66.6 0.6 project.1
  67.2 11.2 %all_to_all.38.in_ref = f32[8,40,128]{2,1,0:T(8,128)S(1)} all-to-all(f32[8,40,128]{2,1,0:T(8,128)S(1)} %get-tuple-element.12), channel_id=1, replica_groups=mesh['y'=8,'z'=8,'x'=4,'c'=2] {'x','c'}, dimensions={0} | all-to-all | bytes 327680 | tf_op jit(solution)/shard_map/all_to_all | solution.py:245
  78.4 9.6 %all_to_all.39.in_ref = bf16[8,32,128]{2,1,0:T(8,128)(2,1)S(1)} all-to-all(bf16[8,32,128]{2,1,0:T(8,128)(2,1)S(1)} %get-tuple-element.13), channel_id=1, replica_groups={{0,8,16,24,32,40,48,56},{64,72,80,88,96,104,112,120},{128,136,144,152,1..., dimensions={0} | all-to-all | bytes 131072 | tf_op jit(solution)/shard_map/all_to_all | solution.py:239
  88.0 10.3 %all_to_all.40.in_ref = f32[8,32,128]{2,1,0:T(8,128)S(1)} all-to-all(f32[8,32,128]{2,1,0:T(8,128)S(1)} %add_copies.4), channel_id=1, replica_groups={{0,64,128,192,256,320,384,448},{8,72,136,200,264,328,392,456},{16,80,14..., dimensions={0} | all-to-all | bytes 262144 | tf_op jit(solution)/shard_map/all_to_all | solution.py:239
  98.3 10.8 %all_to_all.41.in_ref = f32[8,32,128]{2,1,0:T(8,128)S(1)} all-to-all(f32[8,32,128]{2,1,0:T(8,128)S(1)} %add_copies.5), channel_id=1, replica_groups=mesh['y'=8,'z'=8,'x'=4,'c'=2] {'x','c'}, dimensions={0} | all-to-all | bytes 262144 | tf_op jit(solution)/shard_map/all_to_all | solution.py:245
  109.2 4.0 %finish.1 = (bf16[640,1024]{1,0:T(8,128)(2,1)}, f32[32,128]{1,0:T(8,128)}) custom-call(f32[8,32,128]{2,1,0:T(8,128)S(1)} %all_to_all.41.in_ref, f32[8,128]{1,0:T(8,128)S(1)} %get-tuple-element.14.gram_ref, f32[32,640]{1,0:T(8,128)S(1)} %get-tuple-element.15.left_ref, f32[640,1024]{1,0:T(8,128)S(1)} %get-tuple-element.11.merged_ref), custom_call_target="tpu_custom_call" | custom-call | tf_op jit(solution)/shard_map/finish/pallas_call | solution.py:328
  (3 shorter events, 0.1 us)
Async XLA Ops:
  0.6 1.0 copy-start.1
  1.6 0.7 copy-start.3
  3.0 22.2 %copy-start.4 = (bf16[1280,640]{1,0:T(8,128)(2,1)S(1)}, bf16[1280,640]{1,0:T(8,128)(2,1)}, u32[]{:S(2)}) copy-start(bf16[1280,640]{1,0:T(8,128)(2,1)} %act_ref.1) | copy-start | bytes 4915204
  17.4 10.0 %copy-start = (bf16[640,1024]{1,0:T(8,128)(2,1)S(1)}, bf16[640,1024]{1,0:T(8,128)(2,1)}, u32[]{:S(2)}) copy-start(bf16[640,1024]{1,0:T(8,128)(2,1)} %err_ref.1) | copy-start | bytes 3932164
  17.4 10.0 %copy-start.2 = (f32[1024,32]{0,1:T(8,128)S(1)}, f32[1024,32]{0,1:T(8,128)}, u32[]{:S(2)}) copy-start(f32[1024,32]{0,1:T(8,128)} %param.9) | copy-start | bytes 393220
  17.4 10.0 %collective-permute-start = (bf16[4,960,128]{2,1,0:T(8,128)(2,1)S(1)}, bf16[4,960,128]{2,1,0:T(8,128)(2,1)S(1)}, u32[]{:S(2)}, u32[]{:S(2)}) collective-permute-start(bf16[4,960,128]{2,1,0:T(8,128)(2,1)S(1)} %all_to_all.35.own_ref), channel_id=1, source_target_pairs={{0,1},{1,0},{2,3},{3,2},{4,5},{5,4},{6,7},{7,6},{8,9},{9,8},{10,11... | collective-permute-start | bytes 2949128 | tf_op jit(solution)/shard_map/ppermute | solution.py:289

commit v3 on v2

--- a/solution.py
+++ b/solution.py
@@ -72,22 +72,33 @@
     out_ref[...] = jnp.concatenate([kept, spare], axis=0).T.astype(BF16)
 
 
-def merge_kernel(feat_ref, own_ref, other_ref, err_ref, q_ref, merged_ref, left_ref):
-    first = lax.axis_index("c") == 0
-    pieces, kept_count, lanes = own_ref.shape
+def places(side, pieces, lanes):
+    core = lax.axis_index("c")
+    core = core if side == 0 else 1 - core
+    return [pl.multiple_of((2 * piece + core) * lanes, lanes) for piece in range(pieces)]
+
+
+def at_places(ref, starts, lanes):
+    return jnp.concatenate([ref[:, pl.ds(start, lanes)] for start in starts], axis=1)
+
+
+def merge_part(side, feat_ref, cot_ref, err_ref, q_ref, merged_ref):
+    pieces, kept_count, lanes = cot_ref.shape
     rank = q_ref.shape[0]
     features, padded_count = feat_ref.shape
-    q_high, q_low = split(q_ref[...])
+    wide = CHUNK // lanes
+    starts = places(side, pieces, lanes)
     total = jnp.zeros((features, LANES), F32)
-    for piece in range(pieces):
-        own, other = own_ref[piece], other_ref[piece]
-        cots = jnp.concatenate([jnp.where(first, own, other), jnp.where(first, other, own)], axis=1)
+    for chunk in range(pieces // wide):
+        group = range(chunk * wide, (chunk + 1) * wide)
+        spots = [starts[piece] for piece in group]
+        cots = jnp.concatenate([cot_ref[piece] for piece in group], axis=1)
         cots = jnp.concatenate([cots, jnp.zeros((padded_count - kept_count, CHUNK), BF16)], axis=0)
-        here = slice(piece * CHUNK, (piece + 1) * CHUNK)
-        merged = dot(feat_ref[...], cots, ((1,), (0,))) + err_ref[:, here].astype(F32)
-        merged_ref[:, here] = merged
+        old = at_places(err_ref, spots, lanes).astype(F32)
+        merged = dot(feat_ref[...], cots, ((1,), (0,))) + old
+        merged_ref[:, chunk * CHUNK : (chunk + 1) * CHUNK] = merged
         m_high, m_low = split(merged)
-        high, low = q_high[:, here], q_low[:, here]
+        high, low = split(at_places(q_ref, spots, lanes))
         upper = jnp.concatenate([high, high], axis=1)
         lower = jnp.concatenate([low, jnp.zeros_like(low)], axis=1)
         spare = jnp.zeros((LANES - 2 * rank, 2 * CHUNK), BF16)
@@ -96,6 +107,16 @@
             jnp.concatenate([upper, lower, spare], axis=0),
             ((1,), (1,)),
         )
+    return total
+
+
+def merge_own_kernel(feat_ref, own_ref, err_ref, q_ref, merged_ref, total_ref):
+    total_ref[...] = merge_part(0, feat_ref, own_ref, err_ref, q_ref, merged_ref)
+
+
+def merge_other_kernel(feat_ref, other_ref, err_ref, q_ref, total_ref, merged_ref, left_ref):
+    rank = q_ref.shape[0]
+    total = total_ref[...] + merge_part(1, feat_ref, other_ref, err_ref, q_ref, merged_ref)
     turned = total.T
     left = (turned[:rank] + turned[rank : 2 * rank]).astype(BF16)
     for copy in range(left_ref.shape[0]):
@@ -128,7 +149,7 @@
     return jnp.concatenate(blocks, axis=0)
 
 
-def project_kernel(replicas, in_ref, merged_ref, left_ref, out_ref):
+def project_kernel(replicas, in_ref, own_ref, other_ref, left_ref, out_ref):
     rank = left_ref.shape[0]
     pieces, lines, lanes = out_ref.shape
     wide = CHUNK // lanes
@@ -141,14 +162,17 @@
     stack = jnp.concatenate([high, low], axis=0)
     gram = dot(total, total, ((1,), (1,)), lax.Precision.HIGHEST)
     packed = pack(gram, lines - rank)
-    for chunk in range(pieces // wide):
-        m_high, m_low = split(merged_ref[:, chunk * CHUNK : (chunk + 1) * CHUNK])
-        both = dot(stack, m_high, ((1,), (0,)))
-        part = both[:rank] + both[rank:] + dot(high, m_low, ((1,), (0,)))
-        for piece in range(wide):
-            here = chunk * wide + piece
-            out_ref[here, :rank] = part[:, piece * lanes : (piece + 1) * lanes]
-            out_ref[here, rank:] = packed
+    for side, merged_ref in enumerate((own_ref, other_ref)):
+        core = lax.axis_index("c")
+        core = core if side == 0 else 1 - core
+        for chunk in range(merged_ref.shape[1] // CHUNK):
+            m_high, m_low = split(merged_ref[:, chunk * CHUNK : (chunk + 1) * CHUNK])
+            both = dot(stack, m_high, ((1,), (0,)))
+            part = both[:rank] + both[rank:] + dot(high, m_low, ((1,), (0,)))
+            for piece in range(wide):
+                here = 2 * (chunk * wide + piece) + core
+                out_ref[here, :rank] = part[:, piece * lanes : (piece + 1) * lanes]
+                out_ref[here, rank:] = packed
 
 
 def add_blocks_kernel(rank, in_ref, out_ref, gram_ref):
@@ -186,7 +210,20 @@
     return (table / jnp.sqrt(pivots))[:, :rank]
 
 
-def finish_kernel(replicas, in_ref, gram_ref, left_ref, merged_ref, err_hbm, own_ref, q_ref, err_ref, sems):
+def finish_kernel(
+    replicas,
+    in_ref,
+    gram_ref,
+    left_ref,
+    own_merged_ref,
+    other_merged_ref,
+    err_hbm,
+    own_ref,
+    q_ref,
+    stack_ref,
+    err_ref,
+    sems,
+):
     rank, width = q_ref.shape
     inverse = inverse_factor(unpack(gram_ref[...], rank))
     raw = jnp.concatenate([in_ref[piece] for piece in range(in_ref.shape[0])], axis=1)
@@ -198,17 +235,24 @@
     own_ref[...] = dot(inverse, own, ((1,), (0,)), lax.Precision.HIGHEST)
     square = dot(inverse.T, inverse, ((1,), (0,)), lax.Precision.HIGHEST)
     high, low = split(dot(square, raw, ((1,), (0,)), lax.Precision.HIGHEST))
-    stack = jnp.concatenate([high, high, low, jnp.zeros_like(high)], axis=0)
+    stack_ref[...] = jnp.concatenate([high, high, low, jnp.zeros_like(high)], axis=0)
     high, low = split(left_ref[...])
     high = high.astype(F32)
     low = low.astype(F32)
     turned = jnp.concatenate([high, low, high, jnp.zeros_like(high)], axis=0).T.astype(BF16)
+    sides = []
+    for side, merged_ref in enumerate((own_merged_ref, other_merged_ref)):
+        starts = places(side, merged_ref.shape[1] // lanes, lanes)
+        sides.append((merged_ref, starts, at_places(stack_ref, starts, lanes)))
     stores = []
     chunks, rows, _ = err_ref.shape
     for chunk in range(chunks):
         here = slice(chunk * rows, (chunk + 1) * rows)
-        update = dot(turned[here], stack, ((1,), (0,)))
-        err_ref[chunk] = (merged_ref[here] - update).astype(BF16)
+        for merged_ref, starts, stack in sides:
+            fresh = merged_ref[here] - dot(turned[here], stack, ((1,), (0,)))
+            for piece, start in enumerate(starts):
+                block = fresh[:, piece * lanes : (piece + 1) * lanes].astype(BF16)
+                err_ref[chunk, :, pl.ds(start, lanes)] = block
         stores.append(
             pltpu.make_async_copy(
                 err_ref.at[chunk], err_hbm.at[pl.ds(chunk * rows, rows)], sems.at[chunk]
@@ -263,7 +307,6 @@
     replicas = lax.axis_size(DP)
     line_x, across = lax.axis_size("x"), lax.axis_size("z")
     crowd = lax.axis_size(TENSOR)
-    chunks = width // CHUNK
     lines = rank * rank // LANES
     pauses = pause_positions
 
@@ -288,15 +331,30 @@
     cores = lax.axis_size("c")
     other = lax.ppermute(own, "c", [(i, cores - 1 - i) for i in range(cores)])
 
-    merged, left_copies = pl.pallas_call(
-        merge_kernel,
+    turned_q = initial_q.T
+    merged_own, total = pl.pallas_call(
+        merge_own_kernel,
         out_shape=[
-            jax.ShapeDtypeStruct((features, width), F32),
+            jax.ShapeDtypeStruct((features, width // cores), F32),
+            jax.ShapeDtypeStruct((features, LANES), F32),
+        ],
+        compiler_params=params(),
+        cost_estimate=pl.CostEstimate(
+            flops=2 * features * padded_count * width // cores,
+            bytes_accessed=6 * features * width // cores,
+            transcendentals=0,
+        ),
+        name="merge_own",
+    )(kept_features, own, error_old, turned_q)
+    merged_other, left_copies = pl.pallas_call(
+        merge_other_kernel,
+        out_shape=[
+            jax.ShapeDtypeStruct((features, width // cores), F32),
             jax.ShapeDtypeStruct((across, rank, features), BF16),
         ],
         compiler_params=params(),
-        name="merge",
-    )(kept_features, own, other, error_old, initial_q.T)
+        name="merge_other",
+    )(kept_features, other, error_old, turned_q, total)
 
     left_copies = add_copies(to_column(left_copies, 0), lax.axis_size("y"), BF16)
     left_copies = to_column(left_copies, 1)
@@ -309,7 +367,7 @@
         ],
         compiler_params=params(),
         name="project",
-    )(left_copies, merged)
+    )(left_copies, merged_own, merged_other)
 
     q_copies, gram = pl.pallas_call(
         functools.partial(add_blocks_kernel, rank),
@@ -334,12 +392,13 @@
         ],
         scratch_shapes=[
             pltpu.VMEM((rank, width), F32),
+            pltpu.VMEM((4 * rank, width), BF16),
             pltpu.VMEM((parts, LANES, width), BF16),
             pltpu.SemaphoreType.DMA((parts,)),
         ],
         compiler_params=params(),
         name="finish",
-    )(q_pieces, gram, left, merged)
+    )(q_pieces, gram, left, merged_own, merged_other)
     return error_new, own_q.T
 
 

time: 114 us -> 113 us (level)
    pallas_call x1 -> x2, Pallas kernels: 2.59 us -> 3.13 us  [the longest x1 1.81 us: body(): pl.pallas_call(merge_own_kernel, out_shape=[jax.ShapeDtypeStruct((feature...]
  transfers between devices with their start and end apart: 1 -> 1, of which waited for: 1 -> 0; matrix products, arithmetic and copies ran while one was open for 0% -> 0% of each run, Pallas kernels for 1% -> 3%
where the time goes in v3:
time: 113 us
  blocking collectives  92.4 us (82%)
  Pallas kernels  10 us (9%)
  starting transfers between devices  7.79 us (7%)
  local copies, waits for them, and re-layouts  1.66 us (1%)
    all_to_all x4, blocking collectives, to_column(): lax.all_to_all(pieces, axes, split_axis=0, concat_axis=0, tiled=True, axi...  56.4 us
    all_to_all x3, blocking collectives, to_all(): return lax.all_to_all(pieces, axes, split_axis=0, concat_axis=0, tiled=True)  36 us
    ppermute x1, starting transfers between devices, body(): other = lax.ppermute(own, 'c', [(i, cores - 1 - i) for i in range(cores)])  7.79 us
    pallas_call x1, Pallas kernels, body(): pl.pallas_call(functools.partial(finish_kernel, replicas), out_specs=[in_...  4.05 us
  transfers between devices with their start and end apart: 1, of which 0 were waited for; matrix products, arithmetic and copies ran while one was open for 0% of the time, Pallas kernels for 3%

profile of v3, /device:TPU:1, one launch (start us, length us, event | category | flops | bytes accessed | tf_op | source)
XLA Modules:
  0.0 112.7 jit_solution(3191718852389325896)
XLA Ops:
  0.6 0.0 copy-start.2
  0.6 1.0 copy-done.2
  1.6 0.0 copy-start.3
  1.6 0.7 copy-done.3
  2.3 0.8 compact_cotangents.1
  3.0 0.0 copy-start.4
  3.1 14.4 %all_to_all.35.own_ref = bf16[4,960,128]{2,1,0:T(8,128)(2,1)S(1)} all-to-all(bf16[4,960,128]{2,1,0:T(8,128)(2,1)S(1)} %compact_cotangents.1), channel_id=1, replica_groups=mesh['y'=8,'z'=8,'x'=4,'c'=2] {'x'}, dimensions={0} | all-to-all | bytes 1966080 | tf_op jit(solution)/shard_map/all_to_all | solution.py:289
  17.4 0.0 copy-start
  17.4 0.0 copy-start.1
  17.4 7.8 %collective-permute-start = (bf16[4,960,128]{2,1,0:T(8,128)(2,1)S(1)}, bf16[4,960,128]{2,1,0:T(8,128)(2,1)S(1)}, u32[]{:S(2)}, u32[]{:S(2)}) collective-permute-start(bf16[4,960,128]{2,1,0:T(8,128)(2,1)S(1)} %all_to_all.35.own_ref), channel_id=1, source_target_pairs={{0,1},{1,0},{2,3},{3,2},{4,5},{5,4},{6,7},{7,6},{8,9},{9,8},{10,11... | collective-permute-start | bytes 2949128 | tf_op jit(solution)/shard_map/ppermute | solution.py:332
  25.2 0.0 copy-done.4
  25.2 1.4 %compact_features.1.feat_ref = bf16[640,1024]{1,0:T(8,128)(2,1)S(1)} custom-call(s32[320]{0:T(512)S(1)} %copy-done.3, bf16[1280,640]{1,0:T(8,128)(2,1)S(1)} %copy-done.4), custom_call_target="tpu_custom_call" | custom-call | flops 1572864000 | bytes 3276800 | tf_op jit(solution)/shard_map/compact_features/pallas_call | solution.py:320
  26.6 0.0 copy-done
  26.6 0.0 copy-done.1
  26.6 1.8 %merge_own.1 = (f32[640,512]{1,0:T(8,128)S(1)}, f32[640,128]{1,0:T(8,128)S(1)}) custom-call(bf16[640,1024]{1,0:T(8,128)(2,1)S(1)} %compact_features.1.feat_ref, bf16[4,960,128]{2,1,0:T(8,128)(2,1)S(1)} %all_to_all.35.own_ref, bf16[640,1024]{1,0:T(8,128)(2,1)S(1)} %copy-done, f32[32,1024]{1,0:T(8,128)S(1)} %bitcast.2), custom_call_target="tpu_custom_call" | custom-call | flops 671088640 | bytes 1966080 | tf_op jit(solution)/shard_map/merge_own/pallas_call | solution.py:335
  28.5 0.0 collective-permute-done.other_ref
  28.5 1.3 %merge_other.1 = (f32[640,512]{1,0:T(8,128)S(1)}, bf16[8,32,640]{2,1,0:T(8,128)(2,1)S(1)}) custom-call(bf16[640,1024]{1,0:T(8,128)(2,1)S(1)} %compact_features.1.feat_ref, bf16[4,960,128]{2,1,0:T(8,128)(2,1)S(1)} %collective-permute-done.other_ref, bf16[640,1024]{1,0:T(8,128)(2,1)S(1)} %copy-done, f32[32,1024]{1,0:T(8,128)S(1)} %bitcast.3, ...), custom_call_target="tpu_custom_call" | custom-call | tf_op jit(solution)/shard_map/merge_other/pallas_call | solution.py:349
  29.8 16.7 %all_to_all.36.in_ref = bf16[8,32,640]{2,1,0:T(8,128)(2,1)S(1)} all-to-all(bf16[8,32,640]{2,1,0:T(8,128)(2,1)S(1)} %get-tuple-element.13), channel_id=1, replica_groups={{0,8,16,24,32,40,48,56},{64,72,80,88,96,104,112,120},{128,136,144,152,1..., dimensions={0} | all-to-all | bytes 655360 | tf_op jit(solution)/shard_map/all_to_all | solution.py:283
  46.4 0.1 add_copies.3
  46.5 19.9 %all_to_all.37.in_ref = bf16[8,32,640]{2,1,0:T(8,128)(2,1)S(1)} all-to-all(bf16[8,32,640]{2,1,0:T(8,128)(2,1)S(1)} %add_copies.3), channel_id=1, replica_groups={{0,64,128,192,256,320,384,448},{8,72,136,200,264,328,392,456},{16,80,14..., dimensions={0} | all-to-all | bytes 655360 | tf_op jit(solution)/shard_map/all_to_all | solution.py:283
  66.4 0.6 project.1
  67.0 10.8 %all_to_all.38.in_ref = f32[8,40,128]{2,1,0:T(8,128)S(1)} all-to-all(f32[8,40,128]{2,1,0:T(8,128)S(1)} %get-tuple-element.16), channel_id=1, replica_groups=mesh['y'=8,'z'=8,'x'=4,'c'=2] {'x','c'}, dimensions={0} | all-to-all | bytes 327680 | tf_op jit(solution)/shard_map/all_to_all | solution.py:289
  77.8 9.6 %all_to_all.39.in_ref = bf16[8,32,128]{2,1,0:T(8,128)(2,1)S(1)} all-to-all(bf16[8,32,128]{2,1,0:T(8,128)(2,1)S(1)} %get-tuple-element.17), channel_id=1, replica_groups={{0,8,16,24,32,40,48,56},{64,72,80,88,96,104,112,120},{128,136,144,152,1..., dimensions={0} | all-to-all | bytes 131072 | tf_op jit(solution)/shard_map/all_to_all | solution.py:283
  87.4 10.3 %all_to_all.40.in_ref = f32[8,32,128]{2,1,0:T(8,128)S(1)} all-to-all(f32[8,32,128]{2,1,0:T(8,128)S(1)} %add_copies.4), channel_id=1, replica_groups={{0,64,128,192,256,320,384,448},{8,72,136,200,264,328,392,456},{16,80,14..., dimensions={0} | all-to-all | bytes 262144 | tf_op jit(solution)/shard_map/all_to_all | solution.py:283
  97.8 10.8 %all_to_all.41.in_ref = f32[8,32,128]{2,1,0:T(8,128)S(1)} all-to-all(f32[8,32,128]{2,1,0:T(8,128)S(1)} %add_copies.5), channel_id=1, replica_groups=mesh['y'=8,'z'=8,'x'=4,'c'=2] {'x','c'}, dimensions={0} | all-to-all | bytes 262144 | tf_op jit(solution)/shard_map/all_to_all | solution.py:289
  108.6 4.1 %finish.1 = (bf16[640,1024]{1,0:T(8,128)(2,1)}, f32[32,128]{1,0:T(8,128)}) custom-call(f32[8,32,128]{2,1,0:T(8,128)S(1)} %all_to_all.41.in_ref, f32[8,128]{1,0:T(8,128)S(1)} %get-tuple-element.18.gram_ref, f32[32,640]{1,0:T(8,128)S(1)} %get-tuple-element.19.left_ref, f32[640,512]{1,0:T(8,128)S(1)} %get-tuple-element.14.own_ref.own_merged_ref, ...), custom_call_target="tpu_custom_call" | custom-call | tf_op jit(solution)/shard_map/finish/pallas_call | solution.py:386
  (3 shorter events, 0.1 us)
Async XLA Ops:
  0.6 1.0 copy-start.2
  1.6 0.7 copy-start.3
  3.0 22.2 %copy-start.4 = (bf16[1280,640]{1,0:T(8,128)(2,1)S(1)}, bf16[1280,640]{1,0:T(8,128)(2,1)}, u32[]{:S(2)}) copy-start(bf16[1280,640]{1,0:T(8,128)(2,1)} %act_ref.1) | copy-start | bytes 4915204
  17.4 9.2 %copy-start = (bf16[640,1024]{1,0:T(8,128)(2,1)S(1)}, bf16[640,1024]{1,0:T(8,128)(2,1)}, u32[]{:S(2)}) copy-start(bf16[640,1024]{1,0:T(8,128)(2,1)} %err_ref.3) | copy-start | bytes 3932164
  17.4 9.2 %copy-start.1 = (f32[1024,32]{0,1:T(8,128)S(1)}, f32[1024,32]{0,1:T(8,128)}, u32[]{:S(2)}) copy-start(f32[1024,32]{0,1:T(8,128)} %param.9) | copy-start | bytes 393220
  17.4 11.0 %collective-permute-start = (bf16[4,960,128]{2,1,0:T(8,128)(2,1)S(1)}, bf16[4,960,128]{2,1,0:T(8,128)(2,1)S(1)}, u32[]{:S(2)}, u32[]{:S(2)}) collective-permute-start(bf16[4,960,128]{2,1,0:T(8,128)(2,1)S(1)} %all_to_all.35.own_ref), channel_id=1, source_target_pairs={{0,1},{1,0},{2,3},{3,2},{4,5},{5,4},{6,7},{7,6},{8,9},{9,8},{10,11... | collective-permute-start | bytes 2949128 | tf_op jit(solution)/shard_map/ppermute | solution.py:332

commit v4 on v3

--- a/solution.py
+++ b/solution.py
@@ -45,9 +45,8 @@
     return jnp.where(struck > 0.0, -1.0, spot - before)
 
 
-def kept_rows(pauses, values_ref, kept_count):
+def kept_rows(ranks, values_ref, kept_count):
     row_count = values_ref.shape[0]
-    ranks = kept_ranks(pauses, row_count)
     size = kept_count // BLOCKS
     window = size + row_count - kept_count
     blocks = []
@@ -60,14 +59,22 @@
     return jnp.concatenate(blocks, axis=0)
 
 
-def compact_cotangents_kernel(pause_ref, cot_ref, out_ref):
-    kept = kept_rows(pause_ref[...], cot_ref, out_ref.shape[1]).astype(BF16)
+def compact_cotangents_kernel(pause_hbm, cot_hbm, out_ref, pause_ref, cot_ref, sems):
+    pauses = pltpu.make_async_copy(pause_hbm, pause_ref, sems.at[0])
+    cots = pltpu.make_async_copy(cot_hbm, cot_ref, sems.at[1])
+    pauses.start()
+    cots.start()
+    pauses.wait()
+    ranks = kept_ranks(pause_ref[...], cot_ref.shape[0])
+    cots.wait()
+    kept = kept_rows(ranks, cot_ref, out_ref.shape[1]).astype(BF16)
     for copy in range(out_ref.shape[0]):
         out_ref[copy] = kept
 
 
 def compact_features_kernel(kept_count, pause_ref, act_ref, out_ref):
-    kept = kept_rows(pause_ref[...], act_ref, kept_count)
+    ranks = kept_ranks(pause_ref[...], act_ref.shape[0])
+    kept = kept_rows(ranks, act_ref, kept_count)
     spare = jnp.zeros((out_ref.shape[1] - kept_count, kept.shape[1]), F32)
     out_ref[...] = jnp.concatenate([kept, spare], axis=0).T.astype(BF16)
 
@@ -188,6 +195,10 @@
     rank = gram.shape[0]
     row = lax.broadcasted_iota(jnp.int32, (rank, rank), 0)
     col = lax.broadcasted_iota(jnp.int32, (rank, rank), 1)
+    diagonal = jnp.where(row == col, gram, 0.0)
+    scale_row = 1.0 / jnp.sqrt(jnp.sum(diagonal, axis=0, keepdims=True))
+    scale_column = 1.0 / jnp.sqrt(jnp.sum(diagonal, axis=1, keepdims=True))
+    gram = gram * scale_row * scale_column
     spare = jnp.zeros((rank, LANES - 2 * rank), F32)
     table = jnp.concatenate([jnp.where(row == col, 1.0, 0.0), gram, spare], axis=1)
     line = lax.broadcasted_iota(jnp.int32, (rank, LANES), 0)
@@ -196,18 +207,18 @@
         at = rank + k
         column = jnp.broadcast_to(table[:, at : at + 1], (rank, LANES))
         second = jnp.broadcast_to(table[:, at + 1 : at + 2], (rank, LANES))
-        pivot = column[k : k + 1]
-        inverse = 1.0 / pivot
-        slope = column[k + 1 : k + 2] * inverse
-        after = second[k + 1 : k + 2] - slope * second[k : k + 1]
+        pivot, cross = column[k : k + 1], second[k : k + 1]
+        both = pivot * second[k + 1 : k + 2] - cross * cross
+        inverse, inverse_both = 1.0 / pivot, 1.0 / both
         top = table[k : k + 1]
-        bottom = table[k + 1 : k + 2] - slope * top
+        bottom = table[k + 1 : k + 2] - cross * inverse * top
         below = line > k + 1
         upper = jnp.where(below, column * inverse, 0.0)
-        lower = jnp.where(below, second - slope * column, 0.0) * (1.0 / after)
+        lower = jnp.where(below, pivot * second - cross * column, 0.0) * inverse_both
+        after = both * inverse
         table = jnp.where(line == k + 1, bottom, table - upper * top - lower * bottom)
         pivots = jnp.where(line == k, pivot, jnp.where(line == k + 1, after, pivots))
-    return (table / jnp.sqrt(pivots))[:, :rank]
+    return (table / jnp.sqrt(pivots))[:, :rank] * scale_row
 
 
 def finish_kernel(
@@ -267,6 +278,10 @@
     return pl.BlockSpec(memory_space=pltpu.HBM)
 
 
+def kept_in_hbm(x):
+    return pltpu.with_memory_space_constraint(x, pltpu.HBM)
+
+
 def whole(shape):
     return pl.BlockSpec(shape, lambda *_: (0,) * len(shape))
 
@@ -312,10 +327,16 @@
 
     cot_copies = pl.pallas_call(
         compact_cotangents_kernel,
+        in_specs=[in_hbm(), in_hbm()],
+        scratch_shapes=[
+            pltpu.VMEM(pauses.shape, jnp.int32),
+            pltpu.VMEM(cotangents.shape, BF16),
+            pltpu.SemaphoreType.DMA((2,)),
+        ],
         out_shape=jax.ShapeDtypeStruct((line_x, kept_count, lanes), BF16),
         compiler_params=params(),
         name="compact_cotangents",
-    )(pauses, cotangents)
+    )(kept_in_hbm(pauses), kept_in_hbm(cotangents))
     own = to_all(cot_copies, "x")
     kept_features = pl.pallas_call(
         functools.partial(compact_features_kernel, kept_count),

time: 113 us -> 113 us (level)
  local copies, waits for them, and re-layouts: 1.66 us -> 0.02 us
  Pallas kernels: 10 us -> 11.3 us
    unnamed x10 -> x8, local copies, waits for them, and re-layouts: 1.66 us -> 0.02 us
where the time goes in v4:
time: 113 us; the launch traced here: 112 us
  blocking collectives  92.4 us (82%)
  Pallas kernels  11.3 us (10%)
  starting transfers between devices  7.79 us (7%)
    all_to_all x4, blocking collectives, to_column(): lax.all_to_all(pieces, axes, split_axis=0, concat_axis=0, tiled=True, axi...  56.4 us
    all_to_all x3, blocking collectives, to_all(): return lax.all_to_all(pieces, axes, split_axis=0, concat_axis=0, tiled=True)  36 us
    ppermute x1, starting transfers between devices, body(): other = lax.ppermute(own, 'c', [(i, cores - 1 - i) for i in range(cores)])  7.79 us
    pallas_call x1, Pallas kernels, body(): pl.pallas_call(functools.partial(finish_kernel, replicas), out_specs=[in_...  4.55 us
  transfers between devices with their start and end apart: 1, of which 0 were waited for; matrix products, arithmetic and copies ran while one was open for 0% of the time, Pallas kernels for 3%

profile of v4, /device:TPU:1, one launch (start us, length us, event | category | flops | bytes accessed | tf_op | source)
XLA Modules:
  0.0 112.3 jit_solution(10256651896082938171)
XLA Ops:
  0.6 1.5 %compact_cotangents.1 = bf16[4,960,128]{2,1,0:T(8,128)(2,1)S(1)} custom-call(s32[320]{0:T(512)} %pause_hbm.1, bf16[1280,128]{1,0:T(8,128)(2,1)} %cot_hbm.1), custom_call_target="tpu_custom_call" | custom-call | tf_op jit(solution)/shard_map/compact_cotangents/pallas_call | solution.py:328
  2.2 0.0 copy-start.2
  2.2 0.0 copy-start.3
  2.2 14.3 %all_to_all.35.own_ref = bf16[4,960,128]{2,1,0:T(8,128)(2,1)S(1)} all-to-all(bf16[4,960,128]{2,1,0:T(8,128)(2,1)S(1)} %compact_cotangents.1), channel_id=1, replica_groups=mesh['y'=8,'z'=8,'x'=4,'c'=2] {'x'}, dimensions={0} | all-to-all | bytes 1966080 | tf_op jit(solution)/shard_map/all_to_all | solution.py:304
  16.5 0.0 copy-start
  16.5 0.0 copy-start.1
  16.5 7.8 %collective-permute-start = (bf16[4,960,128]{2,1,0:T(8,128)(2,1)S(1)}, bf16[4,960,128]{2,1,0:T(8,128)(2,1)S(1)}, u32[]{:S(2)}, u32[]{:S(2)}) collective-permute-start(bf16[4,960,128]{2,1,0:T(8,128)(2,1)S(1)} %all_to_all.35.own_ref), channel_id=1, source_target_pairs={{0,1},{1,0},{2,3},{3,2},{4,5},{5,4},{6,7},{7,6},{8,9},{9,8},{10,11... | collective-permute-start | bytes 2949128 | tf_op jit(solution)/shard_map/ppermute | solution.py:353
  24.3 0.0 copy-done.2
  24.4 0.0 copy-done.3
  24.4 1.4 %compact_features.1.feat_ref = bf16[640,1024]{1,0:T(8,128)(2,1)S(1)} custom-call(s32[320]{0:T(512)S(1)} %copy-done.2, bf16[1280,640]{1,0:T(8,128)(2,1)S(1)} %copy-done.3), custom_call_target="tpu_custom_call" | custom-call | flops 1572864000 | bytes 3276800 | tf_op jit(solution)/shard_map/compact_features/pallas_call | solution.py:341
  25.8 0.0 copy-done
  25.8 0.0 copy-done.1
  25.8 1.8 %merge_own.1 = (f32[640,512]{1,0:T(8,128)S(1)}, f32[640,128]{1,0:T(8,128)S(1)}) custom-call(bf16[640,1024]{1,0:T(8,128)(2,1)S(1)} %compact_features.1.feat_ref, bf16[4,960,128]{2,1,0:T(8,128)(2,1)S(1)} %all_to_all.35.own_ref, bf16[640,1024]{1,0:T(8,128)(2,1)S(1)} %copy-done, f32[32,1024]{1,0:T(8,128)S(1)} %bitcast.2), custom_call_target="tpu_custom_call" | custom-call | flops 671088640 | bytes 1966080 | tf_op jit(solution)/shard_map/merge_own/pallas_call | solution.py:356
  27.6 0.0 collective-permute-done.other_ref
  27.6 1.3 %merge_other.1 = (f32[640,512]{1,0:T(8,128)S(1)}, bf16[8,32,640]{2,1,0:T(8,128)(2,1)S(1)}) custom-call(bf16[640,1024]{1,0:T(8,128)(2,1)S(1)} %compact_features.1.feat_ref, bf16[4,960,128]{2,1,0:T(8,128)(2,1)S(1)} %collective-permute-done.other_ref, bf16[640,1024]{1,0:T(8,128)(2,1)S(1)} %copy-done, f32[32,1024]{1,0:T(8,128)S(1)} %bitcast.3, ...), custom_call_target="tpu_custom_call" | custom-call | tf_op jit(solution)/shard_map/merge_other/pallas_call | solution.py:370
  28.9 16.7 %all_to_all.36.in_ref = bf16[8,32,640]{2,1,0:T(8,128)(2,1)S(1)} all-to-all(bf16[8,32,640]{2,1,0:T(8,128)(2,1)S(1)} %get-tuple-element.13), channel_id=1, replica_groups={{0,8,16,24,32,40,48,56},{64,72,80,88,96,104,112,120},{128,136,144,152,1..., dimensions={0} | all-to-all | bytes 655360 | tf_op jit(solution)/shard_map/all_to_all | solution.py:298
  45.6 0.1 add_copies.3
  45.6 19.9 %all_to_all.37.in_ref = bf16[8,32,640]{2,1,0:T(8,128)(2,1)S(1)} all-to-all(bf16[8,32,640]{2,1,0:T(8,128)(2,1)S(1)} %add_copies.3), channel_id=1, replica_groups={{0,64,128,192,256,320,384,448},{8,72,136,200,264,328,392,456},{16,80,14..., dimensions={0} | all-to-all | bytes 655360 | tf_op jit(solution)/shard_map/all_to_all | solution.py:298
  65.5 0.6 project.1
  66.1 10.8 %all_to_all.38.in_ref = f32[8,40,128]{2,1,0:T(8,128)S(1)} all-to-all(f32[8,40,128]{2,1,0:T(8,128)S(1)} %get-tuple-element.16), channel_id=1, replica_groups=mesh['y'=8,'z'=8,'x'=4,'c'=2] {'x','c'}, dimensions={0} | all-to-all | bytes 327680 | tf_op jit(solution)/shard_map/all_to_all | solution.py:304
  77.0 9.6 %all_to_all.39.in_ref = bf16[8,32,128]{2,1,0:T(8,128)(2,1)S(1)} all-to-all(bf16[8,32,128]{2,1,0:T(8,128)(2,1)S(1)} %get-tuple-element.17), channel_id=1, replica_groups={{0,8,16,24,32,40,48,56},{64,72,80,88,96,104,112,120},{128,136,144,152,1..., dimensions={0} | all-to-all | bytes 131072 | tf_op jit(solution)/shard_map/all_to_all | solution.py:298
  86.6 10.3 %all_to_all.40.in_ref = f32[8,32,128]{2,1,0:T(8,128)S(1)} all-to-all(f32[8,32,128]{2,1,0:T(8,128)S(1)} %add_copies.4), channel_id=1, replica_groups={{0,64,128,192,256,320,384,448},{8,72,136,200,264,328,392,456},{16,80,14..., dimensions={0} | all-to-all | bytes 262144 | tf_op jit(solution)/shard_map/all_to_all | solution.py:298
  96.9 10.8 %all_to_all.41.in_ref = f32[8,32,128]{2,1,0:T(8,128)S(1)} all-to-all(f32[8,32,128]{2,1,0:T(8,128)S(1)} %add_copies.5), channel_id=1, replica_groups=mesh['y'=8,'z'=8,'x'=4,'c'=2] {'x','c'}, dimensions={0} | all-to-all | bytes 262144 | tf_op jit(solution)/shard_map/all_to_all | solution.py:304
  107.8 4.6 %finish.1 = (bf16[640,1024]{1,0:T(8,128)(2,1)}, f32[32,128]{1,0:T(8,128)}) custom-call(f32[8,32,128]{2,1,0:T(8,128)S(1)} %all_to_all.41.in_ref, f32[8,128]{1,0:T(8,128)S(1)} %get-tuple-element.18.gram_ref, f32[32,640]{1,0:T(8,128)S(1)} %get-tuple-element.19.left_ref, f32[640,512]{1,0:T(8,128)S(1)} %get-tuple-element.14.own_ref.own_merged_ref, ...), custom_call_target="tpu_custom_call" | custom-call | tf_op jit(solution)/shard_map/finish/pallas_call | solution.py:407
  (3 shorter events, 0.0 us)
Async XLA Ops:
  2.2 22.2 %copy-start.2 = (s32[320]{0:T(512)S(1)}, s32[320]{0:T(512)}, u32[]{:S(2)}) copy-start(s32[320]{0:T(512)} %pause_hbm.1) | copy-start | bytes 3844
  2.2 22.2 %copy-start.3 = (bf16[1280,640]{1,0:T(8,128)(2,1)S(1)}, bf16[1280,640]{1,0:T(8,128)(2,1)}, u32[]{:S(2)}) copy-start(bf16[1280,640]{1,0:T(8,128)(2,1)} %act_ref.1) | copy-start | bytes 4915204
  16.5 9.2 %copy-start = (bf16[640,1024]{1,0:T(8,128)(2,1)S(1)}, bf16[640,1024]{1,0:T(8,128)(2,1)}, u32[]{:S(2)}) copy-start(bf16[640,1024]{1,0:T(8,128)(2,1)} %err_ref.3) | copy-start | bytes 3932164
  16.5 9.2 %copy-start.1 = (f32[1024,32]{0,1:T(8,128)S(1)}, f32[1024,32]{0,1:T(8,128)}, u32[]{:S(2)}) copy-start(f32[1024,32]{0,1:T(8,128)} %param.9) | copy-start | bytes 393220
  16.5 11.1 %collective-permute-start = (bf16[4,960,128]{2,1,0:T(8,128)(2,1)S(1)}, bf16[4,960,128]{2,1,0:T(8,128)(2,1)S(1)}, u32[]{:S(2)}, u32[]{:S(2)}) collective-permute-start(bf16[4,960,128]{2,1,0:T(8,128)(2,1)S(1)} %all_to_all.35.own_ref), channel_id=1, source_target_pairs={{0,1},{1,0},{2,3},{3,2},{4,5},{5,4},{6,7},{7,6},{8,9},{9,8},{10,11... | collective-permute-start | bytes 2949128 | tf_op jit(solution)/shard_map/ppermute | solution.py:353

commit v5 on v4

--- a/solution.py
+++ b/solution.py
@@ -195,10 +195,6 @@
     rank = gram.shape[0]
     row = lax.broadcasted_iota(jnp.int32, (rank, rank), 0)
     col = lax.broadcasted_iota(jnp.int32, (rank, rank), 1)
-    diagonal = jnp.where(row == col, gram, 0.0)
-    scale_row = 1.0 / jnp.sqrt(jnp.sum(diagonal, axis=0, keepdims=True))
-    scale_column = 1.0 / jnp.sqrt(jnp.sum(diagonal, axis=1, keepdims=True))
-    gram = gram * scale_row * scale_column
     spare = jnp.zeros((rank, LANES - 2 * rank), F32)
     table = jnp.concatenate([jnp.where(row == col, 1.0, 0.0), gram, spare], axis=1)
     line = lax.broadcasted_iota(jnp.int32, (rank, LANES), 0)
@@ -207,18 +203,18 @@
         at = rank + k
         column = jnp.broadcast_to(table[:, at : at + 1], (rank, LANES))
         second = jnp.broadcast_to(table[:, at + 1 : at + 2], (rank, LANES))
-        pivot, cross = column[k : k + 1], second[k : k + 1]
-        both = pivot * second[k + 1 : k + 2] - cross * cross
-        inverse, inverse_both = 1.0 / pivot, 1.0 / both
+        pivot = column[k : k + 1]
+        inverse = 1.0 / pivot
+        slope = column[k + 1 : k + 2] * inverse
+        after = second[k + 1 : k + 2] - slope * second[k : k + 1]
         top = table[k : k + 1]
-        bottom = table[k + 1 : k + 2] - cross * inverse * top
+        bottom = table[k + 1 : k + 2] - slope * top
         below = line > k + 1
         upper = jnp.where(below, column * inverse, 0.0)
-        lower = jnp.where(below, pivot * second - cross * column, 0.0) * inverse_both
-        after = both * inverse
+        lower = jnp.where(below, second - slope * column, 0.0) * (1.0 / after)
         table = jnp.where(line == k + 1, bottom, table - upper * top - lower * bottom)
         pivots = jnp.where(line == k, pivot, jnp.where(line == k + 1, after, pivots))
-    return (table / jnp.sqrt(pivots))[:, :rank] * scale_row
+    return (table / jnp.sqrt(pivots))[:, :rank]
 
 
 def finish_kernel(

time: 113 us -> 112 us (level)
  no operation moved by 1% of the time
where the time goes in v5:
time: 112 us
  blocking collectives  92.4 us (82%)
  Pallas kernels  10.8 us (10%)
  starting transfers between devices  7.79 us (7%)
    all_to_all x4, blocking collectives, to_column(): lax.all_to_all(pieces, axes, split_axis=0, concat_axis=0, tiled=True, axi...  56.4 us
    all_to_all x3, blocking collectives, to_all(): return lax.all_to_all(pieces, axes, split_axis=0, concat_axis=0, tiled=True)  36 us
    ppermute x1, starting transfers between devices, body(): other = lax.ppermute(own, 'c', [(i, cores - 1 - i) for i in range(cores)])  7.79 us
    pallas_call x1, Pallas kernels, body(): pl.pallas_call(functools.partial(finish_kernel, replicas), out_specs=[in_...  4.04 us
  transfers between devices with their start and end apart: 1, of which 0 were waited for; matrix products, arithmetic and copies ran while one was open for 0% of the time, Pallas kernels for 3%

profile of v5, /device:TPU:1, one launch (start us, length us, event | category | flops | bytes accessed | tf_op | source)
XLA Modules:
  0.0 111.8 jit_solution(1288815595842990951)
XLA Ops:
  0.6 1.5 %compact_cotangents.1 = bf16[4,960,128]{2,1,0:T(8,128)(2,1)S(1)} custom-call(s32[320]{0:T(512)} %pause_hbm.1, bf16[1280,128]{1,0:T(8,128)(2,1)} %cot_hbm.1), custom_call_target="tpu_custom_call" | custom-call | tf_op jit(solution)/shard_map/compact_cotangents/pallas_call | solution.py:324
  2.2 0.0 copy-start.2
  2.2 0.0 copy-start.3
  2.2 14.3 %all_to_all.35.own_ref = bf16[4,960,128]{2,1,0:T(8,128)(2,1)S(1)} all-to-all(bf16[4,960,128]{2,1,0:T(8,128)(2,1)S(1)} %compact_cotangents.1), channel_id=1, replica_groups=mesh['y'=8,'z'=8,'x'=4,'c'=2] {'x'}, dimensions={0} | all-to-all | bytes 1966080 | tf_op jit(solution)/shard_map/all_to_all | solution.py:300
  16.5 0.0 copy-start
  16.5 0.0 copy-start.1
  16.5 7.8 %collective-permute-start = (bf16[4,960,128]{2,1,0:T(8,128)(2,1)S(1)}, bf16[4,960,128]{2,1,0:T(8,128)(2,1)S(1)}, u32[]{:S(2)}, u32[]{:S(2)}) collective-permute-start(bf16[4,960,128]{2,1,0:T(8,128)(2,1)S(1)} %all_to_all.35.own_ref), channel_id=1, source_target_pairs={{0,1},{1,0},{2,3},{3,2},{4,5},{5,4},{6,7},{7,6},{8,9},{9,8},{10,11... | collective-permute-start | bytes 2949128 | tf_op jit(solution)/shard_map/ppermute | solution.py:349
  24.3 0.0 copy-done.2
  24.4 0.0 copy-done.3
  24.4 1.4 %compact_features.1.feat_ref = bf16[640,1024]{1,0:T(8,128)(2,1)S(1)} custom-call(s32[320]{0:T(512)S(1)} %copy-done.2, bf16[1280,640]{1,0:T(8,128)(2,1)S(1)} %copy-done.3), custom_call_target="tpu_custom_call" | custom-call | flops 1572864000 | bytes 3276800 | tf_op jit(solution)/shard_map/compact_features/pallas_call | solution.py:337
  25.8 0.0 copy-done
  25.8 0.0 copy-done.1
  25.8 1.8 %merge_own.1 = (f32[640,512]{1,0:T(8,128)S(1)}, f32[640,128]{1,0:T(8,128)S(1)}) custom-call(bf16[640,1024]{1,0:T(8,128)(2,1)S(1)} %compact_features.1.feat_ref, bf16[4,960,128]{2,1,0:T(8,128)(2,1)S(1)} %all_to_all.35.own_ref, bf16[640,1024]{1,0:T(8,128)(2,1)S(1)} %copy-done, f32[32,1024]{1,0:T(8,128)S(1)} %bitcast.2), custom_call_target="tpu_custom_call" | custom-call | flops 671088640 | bytes 1966080 | tf_op jit(solution)/shard_map/merge_own/pallas_call | solution.py:352
  27.6 0.0 collective-permute-done.other_ref
  27.6 1.3 %merge_other.1 = (f32[640,512]{1,0:T(8,128)S(1)}, bf16[8,32,640]{2,1,0:T(8,128)(2,1)S(1)}) custom-call(bf16[640,1024]{1,0:T(8,128)(2,1)S(1)} %compact_features.1.feat_ref, bf16[4,960,128]{2,1,0:T(8,128)(2,1)S(1)} %collective-permute-done.other_ref, bf16[640,1024]{1,0:T(8,128)(2,1)S(1)} %copy-done, f32[32,1024]{1,0:T(8,128)S(1)} %bitcast.3, ...), custom_call_target="tpu_custom_call" | custom-call | tf_op jit(solution)/shard_map/merge_other/pallas_call | solution.py:366
  28.9 16.7 %all_to_all.36.in_ref = bf16[8,32,640]{2,1,0:T(8,128)(2,1)S(1)} all-to-all(bf16[8,32,640]{2,1,0:T(8,128)(2,1)S(1)} %get-tuple-element.13), channel_id=1, replica_groups={{0,8,16,24,32,40,48,56},{64,72,80,88,96,104,112,120},{128,136,144,152,1..., dimensions={0} | all-to-all | bytes 655360 | tf_op jit(solution)/shard_map/all_to_all | solution.py:294
  45.6 0.1 add_copies.3
  45.6 19.9 %all_to_all.37.in_ref = bf16[8,32,640]{2,1,0:T(8,128)(2,1)S(1)} all-to-all(bf16[8,32,640]{2,1,0:T(8,128)(2,1)S(1)} %add_copies.3), channel_id=1, replica_groups={{0,64,128,192,256,320,384,448},{8,72,136,200,264,328,392,456},{16,80,14..., dimensions={0} | all-to-all | bytes 655360 | tf_op jit(solution)/shard_map/all_to_all | solution.py:294
  65.5 0.6 project.1
  66.1 10.8 %all_to_all.38.in_ref = f32[8,40,128]{2,1,0:T(8,128)S(1)} all-to-all(f32[8,40,128]{2,1,0:T(8,128)S(1)} %get-tuple-element.16), channel_id=1, replica_groups=mesh['y'=8,'z'=8,'x'=4,'c'=2] {'x','c'}, dimensions={0} | all-to-all | bytes 327680 | tf_op jit(solution)/shard_map/all_to_all | solution.py:300
  77.0 9.6 %all_to_all.39.in_ref = bf16[8,32,128]{2,1,0:T(8,128)(2,1)S(1)} all-to-all(bf16[8,32,128]{2,1,0:T(8,128)(2,1)S(1)} %get-tuple-element.17), channel_id=1, replica_groups={{0,8,16,24,32,40,48,56},{64,72,80,88,96,104,112,120},{128,136,144,152,1..., dimensions={0} | all-to-all | bytes 131072 | tf_op jit(solution)/shard_map/all_to_all | solution.py:294
  86.6 10.3 %all_to_all.40.in_ref = f32[8,32,128]{2,1,0:T(8,128)S(1)} all-to-all(f32[8,32,128]{2,1,0:T(8,128)S(1)} %add_copies.4), channel_id=1, replica_groups={{0,64,128,192,256,320,384,448},{8,72,136,200,264,328,392,456},{16,80,14..., dimensions={0} | all-to-all | bytes 262144 | tf_op jit(solution)/shard_map/all_to_all | solution.py:294
  96.9 10.8 %all_to_all.41.in_ref = f32[8,32,128]{2,1,0:T(8,128)S(1)} all-to-all(f32[8,32,128]{2,1,0:T(8,128)S(1)} %add_copies.5), channel_id=1, replica_groups=mesh['y'=8,'z'=8,'x'=4,'c'=2] {'x','c'}, dimensions={0} | all-to-all | bytes 262144 | tf_op jit(solution)/shard_map/all_to_all | solution.py:300
  107.8 4.0 %finish.1 = (bf16[640,1024]{1,0:T(8,128)(2,1)}, f32[32,128]{1,0:T(8,128)}) custom-call(f32[8,32,128]{2,1,0:T(8,128)S(1)} %all_to_all.41.in_ref, f32[8,128]{1,0:T(8,128)S(1)} %get-tuple-element.18.gram_ref, f32[32,640]{1,0:T(8,128)S(1)} %get-tuple-element.19.left_ref, f32[640,512]{1,0:T(8,128)S(1)} %get-tuple-element.14.own_ref.own_merged_ref, ...), custom_call_target="tpu_custom_call" | custom-call | tf_op jit(solution)/shard_map/finish/pallas_call | solution.py:403
  (3 shorter events, 0.0 us)
Async XLA Ops:
  2.2 22.2 %copy-start.2 = (s32[320]{0:T(512)S(1)}, s32[320]{0:T(512)}, u32[]{:S(2)}) copy-start(s32[320]{0:T(512)} %pause_hbm.1) | copy-start | bytes 3844
  2.2 22.2 %copy-start.3 = (bf16[1280,640]{1,0:T(8,128)(2,1)S(1)}, bf16[1280,640]{1,0:T(8,128)(2,1)}, u32[]{:S(2)}) copy-start(bf16[1280,640]{1,0:T(8,128)(2,1)} %act_ref.1) | copy-start | bytes 4915204
  16.5 9.2 %copy-start = (bf16[640,1024]{1,0:T(8,128)(2,1)S(1)}, bf16[640,1024]{1,0:T(8,128)(2,1)}, u32[]{:S(2)}) copy-start(bf16[640,1024]{1,0:T(8,128)(2,1)} %err_ref.3) | copy-start | bytes 3932164
  16.5 9.2 %copy-start.1 = (f32[1024,32]{0,1:T(8,128)S(1)}, f32[1024,32]{0,1:T(8,128)}, u32[]{:S(2)}) copy-start(f32[1024,32]{0,1:T(8,128)} %param.9) | copy-start | bytes 393220
  16.5 11.1 %collective-permute-start = (bf16[4,960,128]{2,1,0:T(8,128)(2,1)S(1)}, bf16[4,960,128]{2,1,0:T(8,128)(2,1)S(1)}, u32[]{:S(2)}, u32[]{:S(2)}) collective-permute-start(bf16[4,960,128]{2,1,0:T(8,128)(2,1)S(1)} %all_to_all.35.own_ref), channel_id=1, source_target_pairs={{0,1},{1,0},{2,3},{3,2},{4,5},{5,4},{6,7},{7,6},{8,9},{9,8},{10,11... | collective-permute-start | bytes 2949128 | tf_op jit(solution)/shard_map/ppermute | solution.py:349

commit v6 on v5

--- a/solution.py
+++ b/solution.py
@@ -59,22 +59,22 @@
     return jnp.concatenate(blocks, axis=0)
 
 
-def compact_cotangents_kernel(pause_hbm, cot_hbm, out_ref, pause_ref, cot_ref, sems):
+def compact_cotangents_kernel(pause_hbm, cot_hbm, out_ref, ranks_ref, pause_ref, cot_ref, sems):
     pauses = pltpu.make_async_copy(pause_hbm, pause_ref, sems.at[0])
     cots = pltpu.make_async_copy(cot_hbm, cot_ref, sems.at[1])
     pauses.start()
     cots.start()
     pauses.wait()
     ranks = kept_ranks(pause_ref[...], cot_ref.shape[0])
+    ranks_ref[...] = ranks
     cots.wait()
     kept = kept_rows(ranks, cot_ref, out_ref.shape[1]).astype(BF16)
     for copy in range(out_ref.shape[0]):
         out_ref[copy] = kept
 
 
-def compact_features_kernel(kept_count, pause_ref, act_ref, out_ref):
-    ranks = kept_ranks(pause_ref[...], act_ref.shape[0])
-    kept = kept_rows(ranks, act_ref, kept_count)
+def compact_features_kernel(kept_count, ranks_ref, act_ref, out_ref):
+    kept = kept_rows(ranks_ref[...], act_ref, kept_count)
     spare = jnp.zeros((out_ref.shape[1] - kept_count, kept.shape[1]), F32)
     out_ref[...] = jnp.concatenate([kept, spare], axis=0).T.astype(BF16)
 
@@ -321,7 +321,7 @@
     lines = rank * rank // LANES
     pauses = pause_positions
 
-    cot_copies = pl.pallas_call(
+    cot_copies, ranks = pl.pallas_call(
         compact_cotangents_kernel,
         in_specs=[in_hbm(), in_hbm()],
         scratch_shapes=[
@@ -329,7 +329,10 @@
             pltpu.VMEM(cotangents.shape, BF16),
             pltpu.SemaphoreType.DMA((2,)),
         ],
-        out_shape=jax.ShapeDtypeStruct((line_x, kept_count, lanes), BF16),
+        out_shape=[
+            jax.ShapeDtypeStruct((line_x, kept_count, lanes), BF16),
+            jax.ShapeDtypeStruct((1, row_count), F32),
+        ],
         compiler_params=params(),
         name="compact_cotangents",
     )(kept_in_hbm(pauses), kept_in_hbm(cotangents))
@@ -344,7 +347,7 @@
             transcendentals=0,
         ),
         name="compact_features",
-    )(pauses, activations)
+    )(ranks, activations)
     cores = lax.axis_size("c")
     other = lax.ppermute(own, "c", [(i, cores - 1 - i) for i in range(cores)])
 
@@ -399,7 +402,8 @@
     q_copies = add_copies(to_column(q_copies, 1), crowd, F32)
     q_pieces = to_all(q_copies, TENSOR)
 
-    parts = features // LANES
+    lines = LANES // 2
+    parts = features // lines
     error_new, own_q = pl.pallas_call(
         functools.partial(finish_kernel, replicas),
         out_specs=[in_hbm(), whole((rank, lanes))],
@@ -410,7 +414,7 @@
         scratch_shapes=[
             pltpu.VMEM((rank, width), F32),
             pltpu.VMEM((4 * rank, width), BF16),
-            pltpu.VMEM((parts, LANES, width), BF16),
+            pltpu.VMEM((parts, lines, width), BF16),
             pltpu.SemaphoreType.DMA((parts,)),
         ],
         compiler_params=params(),

time: 112 us -> 112 us (level)
  no operation moved by 1% of the time
where the time goes in v6:
time: 112 us
  blocking collectives  92.3 us (82%)
  Pallas kernels  10.6 us (9%)
  starting transfers between devices  7.66 us (7%)
    all_to_all x4, blocking collectives, to_column(): lax.all_to_all(pieces, axes, split_axis=0, concat_axis=0, tiled=True, axi...  56.4 us
    all_to_all x3, blocking collectives, to_all(): return lax.all_to_all(pieces, axes, split_axis=0, concat_axis=0, tiled=True)  35.9 us
    ppermute x1, starting transfers between devices, body(): other = lax.ppermute(own, 'c', [(i, cores - 1 - i) for i in range(cores)])  7.66 us
    pallas_call x1, Pallas kernels, body(): pl.pallas_call(functools.partial(finish_kernel, replicas), out_specs=[in_...  4.05 us
  transfers between devices with their start and end apart: 1, of which 0 were waited for; matrix products, arithmetic and copies ran while one was open for 0% of the time, Pallas kernels for 3%

profile of v6, /device:TPU:1, one launch (start us, length us, event | category | flops | bytes accessed | tf_op | source)
XLA Modules:
  0.0 111.5 jit_solution(5717846032268994602)
XLA Ops:
  0.6 0.0 copy-start.2
  0.6 1.7 %compact_cotangents.1 = (bf16[4,960,128]{2,1,0:T(8,128)(2,1)S(1)}, f32[1,1280]{1,0:T(1,128)S(1)}) custom-call(s32[320]{0:T(512)} %pause_hbm.1, bf16[1280,128]{1,0:T(8,128)(2,1)} %cot_hbm.1), custom_call_target="tpu_custom_call" | custom-call | tf_op jit(solution)/shard_map/compact_cotangents/pallas_call | solution.py:324
  2.3 14.2 %all_to_all.35.own_ref = bf16[4,960,128]{2,1,0:T(8,128)(2,1)S(1)} all-to-all(bf16[4,960,128]{2,1,0:T(8,128)(2,1)S(1)} %get-tuple-element.15), channel_id=1, replica_groups=mesh['y'=8,'z'=8,'x'=4,'c'=2] {'x'}, dimensions={0} | all-to-all | bytes 1966080 | tf_op jit(solution)/shard_map/all_to_all | solution.py:300
  16.5 7.7 %collective-permute-start = (bf16[4,960,128]{2,1,0:T(8,128)(2,1)S(1)}, bf16[4,960,128]{2,1,0:T(8,128)(2,1)S(1)}, u32[]{:S(2)}, u32[]{:S(2)}) collective-permute-start(bf16[4,960,128]{2,1,0:T(8,128)(2,1)S(1)} %all_to_all.35.own_ref), channel_id=1, source_target_pairs={{0,1},{1,0},{2,3},{3,2},{4,5},{5,4},{6,7},{7,6},{8,9},{9,8},{10,11... | collective-permute-start | bytes 2949128 | tf_op jit(solution)/shard_map/ppermute | solution.py:352
  24.2 0.0 copy-done.2
  24.2 0.0 copy-start
  24.2 0.0 copy-start.1
  24.2 1.0 compact_features.1.feat_ref
  25.3 0.3 copy-done
  25.5 0.0 copy-done.1
  25.5 1.8 %merge_own.1 = (f32[640,512]{1,0:T(8,128)S(1)}, f32[640,128]{1,0:T(8,128)S(1)}) custom-call(bf16[640,1024]{1,0:T(8,128)(2,1)S(1)} %compact_features.1.feat_ref, bf16[4,960,128]{2,1,0:T(8,128)(2,1)S(1)} %all_to_all.35.own_ref, bf16[640,1024]{1,0:T(8,128)(2,1)S(1)} %copy-done, f32[32,1024]{1,0:T(8,128)S(1)} %bitcast.2), custom_call_target="tpu_custom_call" | custom-call | flops 671088640 | bytes 1966080 | tf_op jit(solution)/shard_map/merge_own/pallas_call | solution.py:355
  27.3 0.0 collective-permute-done.other_ref
  27.3 1.3 %merge_other.1 = (f32[640,512]{1,0:T(8,128)S(1)}, bf16[8,32,640]{2,1,0:T(8,128)(2,1)S(1)}) custom-call(bf16[640,1024]{1,0:T(8,128)(2,1)S(1)} %compact_features.1.feat_ref, bf16[4,960,128]{2,1,0:T(8,128)(2,1)S(1)} %collective-permute-done.other_ref, bf16[640,1024]{1,0:T(8,128)(2,1)S(1)} %copy-done, f32[32,1024]{1,0:T(8,128)S(1)} %bitcast.3, ...), custom_call_target="tpu_custom_call" | custom-call | tf_op jit(solution)/shard_map/merge_other/pallas_call | solution.py:369
  28.7 16.7 %all_to_all.36.in_ref = bf16[8,32,640]{2,1,0:T(8,128)(2,1)S(1)} all-to-all(bf16[8,32,640]{2,1,0:T(8,128)(2,1)S(1)} %get-tuple-element.17), channel_id=1, replica_groups={{0,8,16,24,32,40,48,56},{64,72,80,88,96,104,112,120},{128,136,144,152,1..., dimensions={0} | all-to-all | bytes 655360 | tf_op jit(solution)/shard_map/all_to_all | solution.py:294
  45.3 0.1 add_copies.3
  45.4 19.9 %all_to_all.37.in_ref = bf16[8,32,640]{2,1,0:T(8,128)(2,1)S(1)} all-to-all(bf16[8,32,640]{2,1,0:T(8,128)(2,1)S(1)} %add_copies.3), channel_id=1, replica_groups={{0,64,128,192,256,320,384,448},{8,72,136,200,264,328,392,456},{16,80,14..., dimensions={0} | all-to-all | bytes 655360 | tf_op jit(solution)/shard_map/all_to_all | solution.py:294
  65.2 0.6 project.1
  65.9 10.8 %all_to_all.38.in_ref = f32[8,40,128]{2,1,0:T(8,128)S(1)} all-to-all(f32[8,40,128]{2,1,0:T(8,128)S(1)} %get-tuple-element.20), channel_id=1, replica_groups=mesh['y'=8,'z'=8,'x'=4,'c'=2] {'x','c'}, dimensions={0} | all-to-all | bytes 327680 | tf_op jit(solution)/shard_map/all_to_all | solution.py:300
  76.7 9.6 %all_to_all.39.in_ref = bf16[8,32,128]{2,1,0:T(8,128)(2,1)S(1)} all-to-all(bf16[8,32,128]{2,1,0:T(8,128)(2,1)S(1)} %get-tuple-element.21), channel_id=1, replica_groups={{0,8,16,24,32,40,48,56},{64,72,80,88,96,104,112,120},{128,136,144,152,1..., dimensions={0} | all-to-all | bytes 131072 | tf_op jit(solution)/shard_map/all_to_all | solution.py:294
  86.3 10.3 %all_to_all.40.in_ref = f32[8,32,128]{2,1,0:T(8,128)S(1)} all-to-all(f32[8,32,128]{2,1,0:T(8,128)S(1)} %add_copies.4), channel_id=1, replica_groups={{0,64,128,192,256,320,384,448},{8,72,136,200,264,328,392,456},{16,80,14..., dimensions={0} | all-to-all | bytes 262144 | tf_op jit(solution)/shard_map/all_to_all | solution.py:294
  96.7 10.8 %all_to_all.41.in_ref = f32[8,32,128]{2,1,0:T(8,128)S(1)} all-to-all(f32[8,32,128]{2,1,0:T(8,128)S(1)} %add_copies.5), channel_id=1, replica_groups=mesh['y'=8,'z'=8,'x'=4,'c'=2] {'x','c'}, dimensions={0} | all-to-all | bytes 262144 | tf_op jit(solution)/shard_map/all_to_all | solution.py:300
  107.5 4.0 %finish.1 = (bf16[640,1024]{1,0:T(8,128)(2,1)}, f32[32,128]{1,0:T(8,128)}) custom-call(f32[8,32,128]{2,1,0:T(8,128)S(1)} %all_to_all.41.in_ref, f32[8,128]{1,0:T(8,128)S(1)} %get-tuple-element.22.gram_ref, f32[32,640]{1,0:T(8,128)S(1)} %get-tuple-element.23.left_ref, f32[640,512]{1,0:T(8,128)S(1)} %get-tuple-element.18.own_ref.own_merged_ref, ...), custom_call_target="tpu_custom_call" | custom-call | tf_op jit(solution)/shard_map/finish/pallas_call | solution.py:407
  (3 shorter events, 0.0 us)
Async XLA Ops:
  0.6 23.6 %copy-start.2 = (bf16[1280,640]{1,0:T(8,128)(2,1)S(1)}, bf16[1280,640]{1,0:T(8,128)(2,1)}, u32[]{:S(2)}) copy-start(bf16[1280,640]{1,0:T(8,128)(2,1)} %act_ref.1) | copy-start | bytes 4915204
  16.5 10.8 %collective-permute-start = (bf16[4,960,128]{2,1,0:T(8,128)(2,1)S(1)}, bf16[4,960,128]{2,1,0:T(8,128)(2,1)S(1)}, u32[]{:S(2)}, u32[]{:S(2)}) collective-permute-start(bf16[4,960,128]{2,1,0:T(8,128)(2,1)S(1)} %all_to_all.35.own_ref), channel_id=1, source_target_pairs={{0,1},{1,0},{2,3},{3,2},{4,5},{5,4},{6,7},{7,6},{8,9},{9,8},{10,11... | collective-permute-start | bytes 2949128 | tf_op jit(solution)/shard_map/ppermute | solution.py:352
  24.2 1.3 %copy-start = (bf16[640,1024]{1,0:T(8,128)(2,1)S(1)}, bf16[640,1024]{1,0:T(8,128)(2,1)}, u32[]{:S(2)}) copy-start(bf16[640,1024]{1,0:T(8,128)(2,1)} %err_ref.3) | copy-start | bytes 3932164
  24.2 1.3 %copy-start.1 = (f32[1024,32]{0,1:T(8,128)S(1)}, f32[1024,32]{0,1:T(8,128)}, u32[]{:S(2)}) copy-start(f32[1024,32]{0,1:T(8,128)} %param.9) | copy-start | bytes 393220
